TPU v7x, 32 devices: a whole 2x2x4 slice. The times are simulated.
32 devices in a mesh: section: 4 (over y, core), mp: 2 (over x), dp: 4 (over z).
Axes of the slice: x: 2, y: 2, z: 4, core: 2. Of those that a mesh axis runs over, the one named last changes fastest.
Arguments:
- upstream_grad: bfloat16 [4, 1024, 4096], P('dp', 'mp'), may hold values from -6 to 6
- x_in: bfloat16 [4, 4, 1024, 4096], P('section', 'dp', 'mp'), may hold values from -42 to 42
- ln_gain: float32 [4, 4096], P('section'), may hold values from 0.5 to 2
- ln_bias: float32 [4, 4096], P('section'), may hold values from -1 to 1
- gate_alpha: float32 [4], P('section'), may hold values from 0.4 to 1.5
- w_query: bfloat16 [4, 4096, 512], P('section', None, 'mp'), may hold values from -0.09375 to 0.09375
- w_key: bfloat16 [4, 1024, 512], P('section', None, 'mp'), may hold values from -0.1875 to 0.1875
- w_value: bfloat16 [4, 1024, 512], P('section', None, 'mp'), may hold values from -0.1875 to 0.1875
- w_out: bfloat16 [4, 4096, 512], P('section', None, 'mp'), may hold values from -0.25 to 0.25
- queries: bfloat16 [4, 4, 1024, 512], P('section', 'dp', None, 'mp'), may hold values from -5.5 to 5.5
- keys: bfloat16 [4, 4, 320, 512], P('section', 'dp', None, 'mp'), may hold values from -5.5 to 5.5
- values: bfloat16 [4, 4, 320, 512], P('section', 'dp', None, 'mp'), may hold values from -5 to 5
- image_index: int32 [4, 1024], P('dp'), may hold values from -1 to 4, as said below
- latents: bfloat16 [4, 320, 1024], P('dp'), may hold values from -42 to 42
- res_gain: float32 [1024], replicated, may hold values from 0.5 to 2
- res_bias: float32 [1024], replicated, may hold values from -1 to 1
Outputs:
- input_grads: bfloat16 [4, 4, 1024, 4096], P('section', 'dp', 'mp')
- query_weight_grad: bfloat16 [4, 4096, 512], P('section', 'dp', 'mp')
- key_weight_grad: bfloat16 [4, 1024, 512], P('section', 'dp', 'mp')
- value_weight_grad: bfloat16 [4, 1024, 512], P('section', 'dp', 'mp')
- out_weight_grad: bfloat16 [4, 4096, 512], P('section', 'dp', 'mp')
- latent_grads: float32 [4, 320, 1024], P('dp', ('section', 'mp'))
Inputs may be any that keep to these rules, and one draw needn't show every extreme that they name: `image_index`: along each sequence the index never falls; each sequence holds exactly 5 images, the first one after its first token.
All inputs are finite; a program needn't handle non-finite values.
Results may differ from a plain program's by a relative error of at most 0.03.
Values may be sent and summed in bfloat16 or wider, within the bound.
A program may use at most 128 MiB of HBM per device.

v0:
```python
import math

import jax
import jax.numpy as jnp
from jax import lax
from jax.sharding import PartitionSpec as P

HEAD_DIM = 64
LATENTS = 64
MICRO = 8


def shifted(x, axis, by):
    length = lax.axis_size(axis)
    pairs = [(i, i + by) for i in range(length) if 0 <= i + by < length]
    return lax.ppermute(x, axis, pairs)


def norm_forward(rows, gain, offset):
    mean = jnp.mean(rows, axis=-1, keepdims=True)
    centered = rows - mean
    rstd = lax.rsqrt(jnp.mean(centered * centered, axis=-1, keepdims=True) + 1e-05)
    normed = centered * rstd
    return (normed * gain + offset, normed, rstd)


def norm_back(grad, normed, rstd, gain):
    scaled = grad * gain
    mean_one = jnp.mean(scaled, axis=-1, keepdims=True)
    mean_two = jnp.mean(scaled * normed, axis=-1, keepdims=True)
    return (scaled - mean_one - normed * mean_two) * rstd


def put_block(buffer, update, place, valid):
    former = lax.dynamic_index_in_dim(buffer, place, 0, keepdims=False)
    return lax.dynamic_update_index_in_dim(buffer, jnp.where(valid, update, former), place, 0)


def per_device(
    upstream_grad,
    x_in,
    ln_gain,
    ln_bias,
    gate_alpha,
    w_query,
    w_key,
    w_value,
    w_out,
    queries,
    keys,
    values,
    image_index,
    latents,
    res_gain,
    res_bias,
):
    f32 = jnp.float32
    bf16 = jnp.bfloat16
    sections = lax.axis_size("section")
    ways = lax.axis_size("mp")
    section_at = lax.axis_index("section")
    way_at = lax.axis_index("mp")
    seq_grp, tok_seq, width = upstream_grad.shape
    rows_dev = seq_grp * tok_seq
    block = rows_dev // MICRO
    gathered = ways * block
    local_inner = w_query.shape[2]
    heads_loc = local_inner // HEAD_DIM
    n_vis = keys.shape[2]
    scale = 1.0 / math.sqrt(HEAD_DIM)
    gate = jnp.tanh(gate_alpha[0])
    gain = ln_gain[0]
    offset = ln_bias[0]
    grad_rows = upstream_grad.reshape(rows_dev, width)
    input_rows = x_in[0].reshape(rows_dev, width)
    query_dev = (
        queries[0]
        .reshape(seq_grp, ways, tok_seq, local_inner)
        .transpose(1, 0, 2, 3)
        .reshape(ways, rows_dev, local_inner)
    )
    index_dev = (
        image_index.reshape(seq_grp, ways, tok_seq).transpose(1, 0, 2).reshape(ways, rows_dev)
    )
    image_of = jnp.arange(n_vis) // LATENTS
    key_all = keys[0]
    value_all = values[0]
    w_q = w_query[0]
    w_o = w_out[0]
    first_step = sections - 1 - section_at
    last_section = section_at == sections - 1
    carry_start = (
        jnp.zeros((block, width), bf16),
        jnp.zeros((MICRO, gathered, width), bf16),
        jnp.zeros((MICRO, gathered, width), bf16),
        jnp.zeros((MICRO, gathered, local_inner), bf16),
        jnp.zeros((MICRO, gathered, local_inner), bf16),
        jnp.zeros((seq_grp, n_vis, local_inner), f32),
        jnp.zeros((seq_grp, n_vis, local_inner), f32),
        jnp.zeros((MICRO, block, width), bf16),
    )

    def step(turn, carry):
        sent, norm_buf, grad_buf, attended_buf, query_buf, key_acc, value_acc, result_buf = carry
        received = shifted(sent, "section", -1)
        micro_at = turn - first_step
        valid = (micro_at >= 0) & (micro_at < MICRO)
        place = jnp.clip(micro_at, 0, MICRO - 1)
        start = place * block
        own_grad = lax.dynamic_slice_in_dim(grad_rows, start, block, 0)
        grad_block = jnp.where(last_section, own_grad, received)
        block_in = lax.dynamic_slice_in_dim(input_rows, start, block, 0).astype(f32)
        norm32, normed, rstd = norm_forward(block_in, gain, offset)
        norm_block = norm32.astype(bf16)
        norm_all, grad_all = (
            lax.all_gather(norm_block, "mp", axis=0, tiled=True),
            lax.all_gather(grad_block, "mp", axis=0, tiled=True),
        )
        norm_buf = put_block(norm_buf, norm_all, place, valid)
        seq_at = start // tok_seq
        query_block = lax.dynamic_slice_in_dim(query_dev, start, block, 1).reshape(
            gathered, heads_loc, HEAD_DIM
        )
        index_block = lax.dynamic_slice_in_dim(index_dev, start, block, 1).reshape(gathered)
        key_seq = lax.dynamic_index_in_dim(key_all, seq_at, 0, keepdims=False).reshape(
            n_vis, heads_loc, HEAD_DIM
        )
        value_seq = lax.dynamic_index_in_dim(value_all, seq_at, 0, keepdims=False).reshape(
            n_vis, heads_loc, HEAD_DIM
        )
        scores = (
            jnp.einsum("thd,nhd->htn", query_block, key_seq, preferred_element_type=f32) * scale
        )
        allowed = image_of[None, :] == index_block[:, None]
        has_image = jnp.any(allowed, axis=1)
        top = jnp.max(jnp.where(allowed[None], scores, -1e30), axis=2, keepdims=True)
        top = jnp.where(has_image[None, :, None], top, 0.0)
        expd = jnp.exp(jnp.where(allowed[None], scores - top, -jnp.inf))
        total = jnp.sum(expd, axis=2, keepdims=True) + (1.0 - has_image.astype(f32))[None, :, None]
        probs = expd / total
        probs_b = probs.astype(bf16)
        attended = jnp.einsum(
            "htn,nhd->thd", probs_b, value_seq, preferred_element_type=f32
        ).astype(bf16)
        grad_attended = (gate * jnp.dot(grad_all, w_o, preferred_element_type=f32)).astype(bf16)
        grad_att3 = grad_attended.reshape(gathered, heads_loc, HEAD_DIM)
        grad_probs = jnp.einsum("thd,nhd->htn", grad_att3, value_seq, preferred_element_type=f32)
        inner_sum = jnp.einsum("thd,thd->ht", grad_att3, attended, preferred_element_type=f32)
        grad_scores = (probs * (grad_probs - inner_sum[:, :, None]) * scale).astype(bf16)
        grad_queries = (
            jnp.einsum("htn,nhd->thd", grad_scores, key_seq, preferred_element_type=f32)
            .astype(bf16)
            .reshape(gathered, local_inner)
        )
        key_add = jnp.einsum(
            "htn,thd->nhd", grad_scores, query_block, preferred_element_type=f32
        ).reshape(n_vis, local_inner)
        value_add = jnp.einsum(
            "htn,thd->nhd", probs_b, grad_att3, preferred_element_type=f32
        ).reshape(n_vis, local_inner)
        weight = valid.astype(f32)
        key_acc = lax.dynamic_update_index_in_dim(
            key_acc,
            lax.dynamic_index_in_dim(key_acc, seq_at, 0, keepdims=False) + weight * key_add,
            seq_at,
            0,
        )
        value_acc = lax.dynamic_update_index_in_dim(
            value_acc,
            lax.dynamic_index_in_dim(value_acc, seq_at, 0, keepdims=False) + weight * value_add,
            seq_at,
            0,
        )
        partial_value = lax.dot_general(
            grad_queries, w_q, (((1,), (1,)), ((), ())), preferred_element_type=f32
        )
        summed = lax.psum_scatter(
            partial_value.astype(jnp.bfloat16), "mp", scatter_dimension=0, tiled=True
        ).astype(jnp.float32)
        grad_input = (grad_block.astype(f32) + norm_back(summed, normed, rstd, gain)).astype(bf16)
        grad_buf = put_block(grad_buf, grad_all, place, valid)
        attended_buf = put_block(
            attended_buf, attended.reshape(gathered, local_inner), place, valid
        )
        query_buf = put_block(query_buf, grad_queries, place, valid)
        result_buf = put_block(result_buf, grad_input, place, valid)
        return (
            grad_input,
            norm_buf,
            grad_buf,
            attended_buf,
            query_buf,
            key_acc,
            value_acc,
            result_buf,
        )

    final = lax.fori_loop(0, MICRO + sections - 1, step, carry_start)
    norm_buf, grad_buf, attended_buf, query_buf, key_acc, value_acc, result_buf = final[1:]
    contract_rows = (((0,), (0,)), ((), ()))
    query_grad = lax.dot_general(
        norm_buf.reshape(MICRO * gathered, width),
        query_buf.reshape(MICRO * gathered, local_inner),
        contract_rows,
        preferred_element_type=f32,
    )
    out_grad = gate * lax.dot_general(
        grad_buf.reshape(MICRO * gathered, width),
        attended_buf.reshape(MICRO * gathered, local_inner),
        contract_rows,
        preferred_element_type=f32,
    )
    visual32, lat_normed, lat_rstd = norm_forward(latents.astype(f32), res_gain, res_bias)
    visual = visual32.astype(bf16)
    key_b = key_acc.astype(bf16)
    value_b = value_acc.astype(bf16)
    key_grad = jnp.einsum("snc,sni->ci", visual, key_b, preferred_element_type=f32)
    value_grad = jnp.einsum("snc,sni->ci", visual, value_b, preferred_element_type=f32)
    grads = (
        lax.psum_scatter(
            query_grad.astype(jnp.bfloat16), "dp", scatter_dimension=0, tiled=True
        ).astype(jnp.float32),
        lax.psum_scatter(
            key_grad.astype(jnp.bfloat16), "dp", scatter_dimension=0, tiled=True
        ).astype(jnp.float32),
        lax.psum_scatter(
            value_grad.astype(jnp.bfloat16), "dp", scatter_dimension=0, tiled=True
        ).astype(jnp.float32),
        lax.psum_scatter(
            out_grad.astype(jnp.bfloat16), "dp", scatter_dimension=0, tiled=True
        ).astype(jnp.float32),
    )
    visual_part = jnp.einsum(
        "sni,ci->snc", key_b, w_key[0], preferred_element_type=f32
    ) + jnp.einsum("sni,ci->snc", value_b, w_value[0], preferred_element_type=f32)
    visual_sum = lax.psum_scatter(visual_part, ("section", "mp"), scatter_dimension=1, tiled=True)
    share = visual_sum.shape[1]
    own_start = (section_at * ways + way_at) * share
    own_normed = lax.dynamic_slice_in_dim(lat_normed, own_start, share, 1)
    own_rstd = lax.dynamic_slice_in_dim(lat_rstd, own_start, share, 1)
    latent_grads = norm_back(visual_sum, own_normed, own_rstd, res_gain)
    input_grads = result_buf.reshape(seq_grp, tok_seq, width)[None]
    return (
        input_grads,
        grads[0].astype(bf16)[None],
        grads[1].astype(bf16)[None],
        grads[2].astype(bf16)[None],
        grads[3].astype(bf16)[None],
        latent_grads,
    )


def solution(mesh):
    in_specs = (
        P("dp", "mp", None),
        P("section", "dp", "mp", None),
        P("section", None),
        P("section", None),
        P("section"),
        P("section", None, "mp"),
        P("section", None, "mp"),
        P("section", None, "mp"),
        P("section", None, "mp"),
        P("section", "dp", None, "mp"),
        P("section", "dp", None, "mp"),
        P("section", "dp", None, "mp"),
        P("dp", None),
        P("dp", None, None),
        P(),
        P(),
    )
    out_specs = (
        P("section", "dp", "mp", None),
        P("section", "dp", "mp"),
        P("section", "dp", "mp"),
        P("section", "dp", "mp"),
        P("section", "dp", "mp"),
        P("dp", ("section", "mp"), None),
    )
    return jax.shard_map(
        per_device, mesh=mesh, in_specs=in_specs, out_specs=out_specs, check_vma=False
    )
```

profile of v0, /device:TPU:0, one launch (start us, length us, event | category | flops | bytes accessed | tf_op | source)
XLA Modules:
  0.0 1209.7 jit_solution(8304638562323485449)
XLA Ops:
  26.3 998.3 %while.28 = (s32[]{:T(128)}, bf16[64,4096]{1,0:T(8,128)(2,1)}, bf16[8,128,4096]{2,1,0:T(8,128)(2,1)}, bf16[8,128,4096]{2,1,0:T(8,128)(2,1)}, bf16[8,128,256]{1,2...) while((s32[]{:T(128)}, bf16[64,4096]{1,0:T(8,128)(2,1)}, ...), condition=%wide.region_9.10_spmd.clone, body=%wide.region_0.9_spmd.clone.sunk | while | flops 677005504 | bytes 78738784 | solution.py:198
  38.4 23.2 %all-gather.3.cloned.1.call-done = bf16[128,4096]{1,0:T(8,128)(2,1)} async-done(((bf16[64,4096]{1,0:T(8,128)(2,1)}), bf16[128,4096]{1,0:T(8,128)(2,1)}) %all-gather.3.cloned.1.call-update) | async-done | bytes 1048592 | tf_op jit(solution)/shard_map/while/body/eval_jaxpr/all_gather | solution.py:117
  97.3 18.9 %all-gather.5.cloned.1.call-done = bf16[128,4096]{1,0:T(8,128)(2,1)} async-done(((bf16[64,4096]{1,0:T(8,128)(2,1)}), bf16[128,4096]{1,0:T(8,128)(2,1)}) %all-gather.5.cloned.1.call-update) | async-done | bytes 1048592 | tf_op jit(solution)/shard_map/while/body/eval_jaxpr/all_gather | solution.py:116
  130.6 20.5 %all-gather.3.cloned.1.call-done = bf16[128,4096]{1,0:T(8,128)(2,1)} async-done(((bf16[64,4096]{1,0:T(8,128)(2,1)}), bf16[128,4096]{1,0:T(8,128)(2,1)}) %all-gather.3.cloned.1.call-update) | async-done | bytes 1048592 | tf_op jit(solution)/shard_map/while/body/eval_jaxpr/all_gather | solution.py:117
  186.8 18.9 %all-gather.5.cloned.1.call-done = bf16[128,4096]{1,0:T(8,128)(2,1)} async-done(((bf16[64,4096]{1,0:T(8,128)(2,1)}), bf16[128,4096]{1,0:T(8,128)(2,1)}) %all-gather.5.cloned.1.call-update) | async-done | bytes 1048592 | tf_op jit(solution)/shard_map/while/body/eval_jaxpr/all_gather | solution.py:116
  220.1 21.7 %all-gather.3.cloned.1.call-done = bf16[128,4096]{1,0:T(8,128)(2,1)} async-done(((bf16[64,4096]{1,0:T(8,128)(2,1)}), bf16[128,4096]{1,0:T(8,128)(2,1)}) %all-gather.3.cloned.1.call-update) | async-done | bytes 1048592 | tf_op jit(solution)/shard_map/while/body/eval_jaxpr/all_gather | solution.py:117
  277.5 18.9 %all-gather.5.cloned.1.call-done = bf16[128,4096]{1,0:T(8,128)(2,1)} async-done(((bf16[64,4096]{1,0:T(8,128)(2,1)}), bf16[128,4096]{1,0:T(8,128)(2,1)}) %all-gather.5.cloned.1.call-update) | async-done | bytes 1048592 | tf_op jit(solution)/shard_map/while/body/eval_jaxpr/all_gather | solution.py:116
  310.8 21.7 %all-gather.3.cloned.1.call-done = bf16[128,4096]{1,0:T(8,128)(2,1)} async-done(((bf16[64,4096]{1,0:T(8,128)(2,1)}), bf16[128,4096]{1,0:T(8,128)(2,1)}) %all-gather.3.cloned.1.call-update) | async-done | bytes 1048592 | tf_op jit(solution)/shard_map/while/body/eval_jaxpr/all_gather | solution.py:117
  368.2 18.9 %all-gather.5.cloned.1.call-done = bf16[128,4096]{1,0:T(8,128)(2,1)} async-done(((bf16[64,4096]{1,0:T(8,128)(2,1)}), bf16[128,4096]{1,0:T(8,128)(2,1)}) %all-gather.5.cloned.1.call-update) | async-done | bytes 1048592 | tf_op jit(solution)/shard_map/while/body/eval_jaxpr/all_gather | solution.py:116
  402.7 20.5 %all-gather.3.cloned.1.call-done = bf16[128,4096]{1,0:T(8,128)(2,1)} async-done(((bf16[64,4096]{1,0:T(8,128)(2,1)}), bf16[128,4096]{1,0:T(8,128)(2,1)}) %all-gather.3.cloned.1.call-update) | async-done | bytes 1048592 | tf_op jit(solution)/shard_map/while/body/eval_jaxpr/all_gather | solution.py:117
  441.7 12.0 reduce-scatter.17.cloned.1.call-done
  458.9 18.9 %all-gather.5.cloned.1.call-done = bf16[128,4096]{1,0:T(8,128)(2,1)} async-done(((bf16[64,4096]{1,0:T(8,128)(2,1)}), bf16[128,4096]{1,0:T(8,128)(2,1)}) %all-gather.5.cloned.1.call-update) | async-done | bytes 1048592 | tf_op jit(solution)/shard_map/while/body/eval_jaxpr/all_gather | solution.py:116
  493.4 20.5 %all-gather.3.cloned.1.call-done = bf16[128,4096]{1,0:T(8,128)(2,1)} async-done(((bf16[64,4096]{1,0:T(8,128)(2,1)}), bf16[128,4096]{1,0:T(8,128)(2,1)}) %all-gather.3.cloned.1.call-update) | async-done | bytes 1048592 | tf_op jit(solution)/shard_map/while/body/eval_jaxpr/all_gather | solution.py:117
  549.7 18.9 %all-gather.5.cloned.1.call-done = bf16[128,4096]{1,0:T(8,128)(2,1)} async-done(((bf16[64,4096]{1,0:T(8,128)(2,1)}), bf16[128,4096]{1,0:T(8,128)(2,1)}) %all-gather.5.cloned.1.call-update) | async-done | bytes 1048592 | tf_op jit(solution)/shard_map/while/body/eval_jaxpr/all_gather | solution.py:116
  584.1 20.5 %all-gather.3.cloned.1.call-done = bf16[128,4096]{1,0:T(8,128)(2,1)} async-done(((bf16[64,4096]{1,0:T(8,128)(2,1)}), bf16[128,4096]{1,0:T(8,128)(2,1)}) %all-gather.3.cloned.1.call-update) | async-done | bytes 1048592 | tf_op jit(solution)/shard_map/while/body/eval_jaxpr/all_gather | solution.py:117
  640.4 18.9 %all-gather.5.cloned.1.call-done = bf16[128,4096]{1,0:T(8,128)(2,1)} async-done(((bf16[64,4096]{1,0:T(8,128)(2,1)}), bf16[128,4096]{1,0:T(8,128)(2,1)}) %all-gather.5.cloned.1.call-update) | async-done | bytes 1048592 | tf_op jit(solution)/shard_map/while/body/eval_jaxpr/all_gather | solution.py:116
  674.8 20.5 %all-gather.3.cloned.1.call-done = bf16[128,4096]{1,0:T(8,128)(2,1)} async-done(((bf16[64,4096]{1,0:T(8,128)(2,1)}), bf16[128,4096]{1,0:T(8,128)(2,1)}) %all-gather.3.cloned.1.call-update) | async-done | bytes 1048592 | tf_op jit(solution)/shard_map/while/body/eval_jaxpr/all_gather | solution.py:117
  731.1 18.9 %all-gather.5.cloned.1.call-done = bf16[128,4096]{1,0:T(8,128)(2,1)} async-done(((bf16[64,4096]{1,0:T(8,128)(2,1)}), bf16[128,4096]{1,0:T(8,128)(2,1)}) %all-gather.5.cloned.1.call-update) | async-done | bytes 1048592 | tf_op jit(solution)/shard_map/while/body/eval_jaxpr/all_gather | solution.py:116
  765.5 20.5 %all-gather.3.cloned.1.call-done = bf16[128,4096]{1,0:T(8,128)(2,1)} async-done(((bf16[64,4096]{1,0:T(8,128)(2,1)}), bf16[128,4096]{1,0:T(8,128)(2,1)}) %all-gather.3.cloned.1.call-update) | async-done | bytes 1048592 | tf_op jit(solution)/shard_map/while/body/eval_jaxpr/all_gather | solution.py:117
  804.5 12.0 reduce-scatter.17.cloned.1.call-done
  821.8 18.9 %all-gather.5.cloned.1.call-done = bf16[128,4096]{1,0:T(8,128)(2,1)} async-done(((bf16[64,4096]{1,0:T(8,128)(2,1)}), bf16[128,4096]{1,0:T(8,128)(2,1)}) %all-gather.5.cloned.1.call-update) | async-done | bytes 1048592 | tf_op jit(solution)/shard_map/while/body/eval_jaxpr/all_gather | solution.py:116
  856.3 20.5 %all-gather.3.cloned.1.call-done = bf16[128,4096]{1,0:T(8,128)(2,1)} async-done(((bf16[64,4096]{1,0:T(8,128)(2,1)}), bf16[128,4096]{1,0:T(8,128)(2,1)}) %all-gather.3.cloned.1.call-update) | async-done | bytes 1048592 | tf_op jit(solution)/shard_map/while/body/eval_jaxpr/all_gather | solution.py:117
  895.3 12.0 reduce-scatter.17.cloned.1.call-done
  912.5 18.9 %all-gather.5.cloned.1.call-done = bf16[128,4096]{1,0:T(8,128)(2,1)} async-done(((bf16[64,4096]{1,0:T(8,128)(2,1)}), bf16[128,4096]{1,0:T(8,128)(2,1)}) %all-gather.5.cloned.1.call-update) | async-done | bytes 1048592 | tf_op jit(solution)/shard_map/while/body/eval_jaxpr/all_gather | solution.py:116
  947.0 20.5 %all-gather.3.cloned.1.call-done = bf16[128,4096]{1,0:T(8,128)(2,1)} async-done(((bf16[64,4096]{1,0:T(8,128)(2,1)}), bf16[128,4096]{1,0:T(8,128)(2,1)}) %all-gather.3.cloned.1.call-update) | async-done | bytes 1048592 | tf_op jit(solution)/shard_map/while/body/eval_jaxpr/all_gather | solution.py:117
  986.0 12.0 reduce-scatter.17.cloned.1.call-done
  1003.2 18.9 %all-gather.5.cloned.1.call-done = bf16[128,4096]{1,0:T(8,128)(2,1)} async-done(((bf16[64,4096]{1,0:T(8,128)(2,1)}), bf16[128,4096]{1,0:T(8,128)(2,1)}) %all-gather.5.cloned.1.call-update) | async-done | bytes 1048592 | tf_op jit(solution)/shard_map/while/body/eval_jaxpr/all_gather | solution.py:116
  1048.0 16.6 %reduce-scatter.15.cloned.1.call-done = f32[1,40,1024]{2,1,0:T(8,128)} async-done(((f32[1,320,1024]{2,1,0:T(8,128)}), f32[1,40,1024]{2,1,0:T(8,128)}) %reduce-scatter.15.cloned.1.call-update) | async-done | bytes 163856 | tf_op jit(solution)/shard_map/reduce_scatter | solution.py:236
  1067.3 21.6 %reduce-scatter.9.cloned.1.call-done = bf16[256,256]{1,0:T(8,128)(2,1)} async-done(((bf16[1024,256]{1,0:T(8,128)(2,1)}), bf16[256,256]{1,0:T(8,128)(2,1)}) %reduce-scatter.9.cloned.1.call-update) | async-done | bytes 131088 | tf_op jit(solution)/shard_map/reduce_scatter | solution.py:223
  1088.9 22.7 %reduce-scatter.11.cloned.1.call-done = bf16[256,256]{1,0:T(8,128)(2,1)} async-done(((bf16[1024,256]{1,0:T(8,128)(2,1)}), bf16[256,256]{1,0:T(8,128)(2,1)}) %reduce-scatter.11.cloned.1.call-update) | async-done | bytes 131088 | tf_op jit(solution)/shard_map/reduce_scatter | solution.py:226
  1111.6 44.8 %reduce-scatter.13.cloned.1.call-done = bf16[1024,256]{1,0:T(8,128)(2,1)} async-done(((bf16[4096,256]{1,0:T(8,128)(2,1)}), bf16[1024,256]{1,0:T(8,128)(2,1)}) %reduce-scatter.13.cloned.1.call-update) | async-done | bytes 524304 | tf_op jit(solution)/shard_map/reduce_scatter | solution.py:229
  1156.4 45.7 %reduce-scatter.7.cloned.1.call-done = bf16[1024,256]{1,0:T(8,128)(2,1)} async-done(((bf16[4096,256]{1,0:T(8,128)(2,1)}), bf16[1024,256]{1,0:T(8,128)(2,1)}) %reduce-scatter.7.cloned.1.call-update) | async-done | bytes 524304 | tf_op jit(solution)/shard_map/reduce_scatter | solution.py:220
  (1022 shorter events, 551.7 us)
Async XLA Ops:
  26.3 35.3 %all-gather.3.cloned.1.call-start = ((), (), s32[]{:S(2)}) async-start(), calls=%async_computation.11 | async-start | bytes 1572864 | tf_op jit(solution)/shard_map/while/body/eval_jaxpr/all_gather | solution.py:117
  32.9 59.3 %reduce-scatter.17.cloned.1.call-start = ((), (), s32[]{:S(2)}) async-start(), calls=%async_computation.12 | async-start | bytes 1572864 | tf_op jit(solution)/shard_map/while/body/eval_jaxpr/reduce_scatter | solution.py:177
  71.7 44.6 %all-gather.5.cloned.1.call-start = ((), (), s32[]{:S(2)}) async-start(), calls=%async_computation.13 | async-start | bytes 1572864 | tf_op jit(solution)/shard_map/while/body/eval_jaxpr/all_gather | solution.py:116
  125.0 56.6 %reduce-scatter.17.cloned.1.call-start = ((), (), s32[]{:S(2)}) async-start(), calls=%async_computation.12 | async-start | bytes 1572864 | tf_op jit(solution)/shard_map/while/body/eval_jaxpr/reduce_scatter | solution.py:177
  161.1 44.6 %all-gather.5.cloned.1.call-start = ((), (), s32[]{:S(2)}) async-start(), calls=%async_computation.13 | async-start | bytes 1572864 | tf_op jit(solution)/shard_map/while/body/eval_jaxpr/all_gather | solution.py:116
  206.9 34.9 %all-gather.3.cloned.1.call-start = ((), (), s32[]{:S(2)}) async-start(), calls=%async_computation.11 | async-start | bytes 1572864 | tf_op jit(solution)/shard_map/while/body/eval_jaxpr/all_gather | solution.py:117
  214.5 57.8 %reduce-scatter.17.cloned.1.call-start = ((), (), s32[]{:S(2)}) async-start(), calls=%async_computation.12 | async-start | bytes 1572864 | tf_op jit(solution)/shard_map/while/body/eval_jaxpr/reduce_scatter | solution.py:177
  251.8 44.6 %all-gather.5.cloned.1.call-start = ((), (), s32[]{:S(2)}) async-start(), calls=%async_computation.13 | async-start | bytes 1572864 | tf_op jit(solution)/shard_map/while/body/eval_jaxpr/all_gather | solution.py:116
  297.6 34.9 %all-gather.3.cloned.1.call-start = ((), (), s32[]{:S(2)}) async-start(), calls=%async_computation.11 | async-start | bytes 1572864 | tf_op jit(solution)/shard_map/while/body/eval_jaxpr/all_gather | solution.py:117
  305.2 57.8 %reduce-scatter.17.cloned.1.call-start = ((), (), s32[]{:S(2)}) async-start(), calls=%async_computation.12 | async-start | bytes 1572864 | tf_op jit(solution)/shard_map/while/body/eval_jaxpr/reduce_scatter | solution.py:177
  342.5 44.6 %all-gather.5.cloned.1.call-start = ((), (), s32[]{:S(2)}) async-start(), calls=%async_computation.13 | async-start | bytes 1572864 | tf_op jit(solution)/shard_map/while/body/eval_jaxpr/all_gather | solution.py:116
  397.1 56.6 %reduce-scatter.17.cloned.1.call-start = ((), (), s32[]{:S(2)}) async-start(), calls=%async_computation.12 | async-start | bytes 1572864 | tf_op jit(solution)/shard_map/while/body/eval_jaxpr/reduce_scatter | solution.py:177
  433.3 44.6 %all-gather.5.cloned.1.call-start = ((), (), s32[]{:S(2)}) async-start(), calls=%async_computation.13 | async-start | bytes 1572864 | tf_op jit(solution)/shard_map/while/body/eval_jaxpr/all_gather | solution.py:116
  487.9 56.6 %reduce-scatter.17.cloned.1.call-start = ((), (), s32[]{:S(2)}) async-start(), calls=%async_computation.12 | async-start | bytes 1572864 | tf_op jit(solution)/shard_map/while/body/eval_jaxpr/reduce_scatter | solution.py:177
  524.0 44.6 %all-gather.5.cloned.1.call-start = ((), (), s32[]{:S(2)}) async-start(), calls=%async_computation.13 | async-start | bytes 1572864 | tf_op jit(solution)/shard_map/while/body/eval_jaxpr/all_gather | solution.py:116
  578.6 56.6 %reduce-scatter.17.cloned.1.call-start = ((), (), s32[]{:S(2)}) async-start(), calls=%async_computation.12 | async-start | bytes 1572864 | tf_op jit(solution)/shard_map/while/body/eval_jaxpr/reduce_scatter | solution.py:177
  614.7 44.6 %all-gather.5.cloned.1.call-start = ((), (), s32[]{:S(2)}) async-start(), calls=%async_computation.13 | async-start | bytes 1572864 | tf_op jit(solution)/shard_map/while/body/eval_jaxpr/all_gather | solution.py:116
  669.3 56.6 %reduce-scatter.17.cloned.1.call-start = ((), (), s32[]{:S(2)}) async-start(), calls=%async_computation.12 | async-start | bytes 1572864 | tf_op jit(solution)/shard_map/while/body/eval_jaxpr/reduce_scatter | solution.py:177
  705.4 44.6 %all-gather.5.cloned.1.call-start = ((), (), s32[]{:S(2)}) async-start(), calls=%async_computation.13 | async-start | bytes 1572864 | tf_op jit(solution)/shard_map/while/body/eval_jaxpr/all_gather | solution.py:116
  752.4 33.7 %all-gather.3.cloned.1.call-start = ((), (), s32[]{:S(2)}) async-start(), calls=%async_computation.11 | async-start | bytes 1572864 | tf_op jit(solution)/shard_map/while/body/eval_jaxpr/all_gather | solution.py:117
  760.0 56.6 %reduce-scatter.17.cloned.1.call-start = ((), (), s32[]{:S(2)}) async-start(), calls=%async_computation.12 | async-start | bytes 1572864 | tf_op jit(solution)/shard_map/while/body/eval_jaxpr/reduce_scatter | solution.py:177
  796.1 44.6 %all-gather.5.cloned.1.call-start = ((), (), s32[]{:S(2)}) async-start(), calls=%async_computation.13 | async-start | bytes 1572864 | tf_op jit(solution)/shard_map/while/body/eval_jaxpr/all_gather | solution.py:116
  843.1 33.7 %all-gather.3.cloned.1.call-start = ((), (), s32[]{:S(2)}) async-start(), calls=%async_computation.11 | async-start | bytes 1572864 | tf_op jit(solution)/shard_map/while/body/eval_jaxpr/all_gather | solution.py:117
  850.7 56.6 %reduce-scatter.17.cloned.1.call-start = ((), (), s32[]{:S(2)}) async-start(), calls=%async_computation.12 | async-start | bytes 1572864 | tf_op jit(solution)/shard_map/while/body/eval_jaxpr/reduce_scatter | solution.py:177
  886.8 44.6 %all-gather.5.cloned.1.call-start = ((), (), s32[]{:S(2)}) async-start(), calls=%async_computation.13 | async-start | bytes 1572864 | tf_op jit(solution)/shard_map/while/body/eval_jaxpr/all_gather | solution.py:116
  941.4 56.6 %reduce-scatter.17.cloned.1.call-start = ((), (), s32[]{:S(2)}) async-start(), calls=%async_computation.12 | async-start | bytes 1572864 | tf_op jit(solution)/shard_map/while/body/eval_jaxpr/reduce_scatter | solution.py:177
  977.5 44.6 %all-gather.5.cloned.1.call-start = ((), (), s32[]{:S(2)}) async-start(), calls=%async_computation.13 | async-start | bytes 1572864 | tf_op jit(solution)/shard_map/while/body/eval_jaxpr/all_gather | solution.py:116
  1024.6 40.0 %reduce-scatter.15.cloned.1.call-start = ((), (), s32[]{:S(2)}) async-start(), calls=%async_computation.10 | async-start | bytes 1474560 | tf_op jit(solution)/shard_map/reduce_scatter | solution.py:236
  1027.7 61.2 %reduce-scatter.9.cloned.1.call-start = ((), (), s32[]{:S(2)}) async-start(), calls=%async_computation.7 | async-start | bytes 655360 | tf_op jit(solution)/shard_map/reduce_scatter | solution.py:223
  1030.1 81.5 %reduce-scatter.11.cloned.1.call-start = ((), (), s32[]{:S(2)}) async-start(), calls=%async_computation.8 | async-start | bytes 655360 | tf_op jit(solution)/shard_map/reduce_scatter | solution.py:226
  1031.6 124.8 %reduce-scatter.13.cloned.1.call-start = ((), (), s32[]{:S(2)}) async-start(), calls=%async_computation.9 | async-start | bytes 2621440 | tf_op jit(solution)/shard_map/reduce_scatter | solution.py:229
  1039.4 162.8 %reduce-scatter.7.cloned.1.call-start = ((), (), s32[]{:S(2)}) async-start(), calls=%async_computation.6 | async-start | bytes 2621440 | tf_op jit(solution)/shard_map/reduce_scatter | solution.py:220
  (269 other events, 3884.1 us)
Sparse Core Ops, SparseCore 0:
  33.0 28.5 all-gather.2
  71.8 20.3 reduce-scatter.16
  94.9 21.2 all-gather.4
  125.1 25.8 all-gather.2
  161.2 20.3 reduce-scatter.16
  184.3 21.2 all-gather.4
  214.6 27.1 all-gather.2
  251.9 20.3 reduce-scatter.16
  275.0 21.2 all-gather.4
  305.3 27.1 all-gather.2
  342.7 20.3 reduce-scatter.16
  365.8 21.2 all-gather.4
  397.3 25.8 all-gather.2
  433.4 20.3 reduce-scatter.16
  456.5 21.2 all-gather.4
  488.0 25.8 all-gather.2
  524.1 20.3 reduce-scatter.16
  547.2 21.2 all-gather.4
  578.7 25.8 all-gather.2
  614.8 20.3 reduce-scatter.16
  637.9 21.2 all-gather.4
  669.4 25.8 all-gather.2
  705.5 20.3 reduce-scatter.16
  728.6 21.2 all-gather.4
  760.1 25.8 all-gather.2
  796.2 20.3 reduce-scatter.16
  819.3 21.2 all-gather.4
  850.8 25.9 all-gather.2
  886.9 20.3 reduce-scatter.16
  910.0 21.2 all-gather.4
  941.5 25.8 all-gather.2
  1000.7 21.2 all-gather.4
  (1 shorter events, 20.3 us)
Sparse Core Ops, SparseCore 1:
  1028.3 36.3 reduce-scatter.14
  1067.3 21.5 reduce-scatter.8
  1091.6 19.9 reduce-scatter.10
  1114.5 41.8 reduce-scatter.12
  1159.4 42.7 reduce-scatter.6
where the time goes:
time: 1220 us; the launch traced here: 1210 us
  waiting for transfers between devices  722 us (59%)
  other arithmetic  203 us (17%)
  matrix products  132 us (11%)
  local copies, waits for them, and re-layouts  116 us (10%)
  between operations  16.5 us (1%)
  starting transfers between devices  15.6 us (1%)
    all_gather x11, waiting for transfers between devices, step(): lax.all_gather(grad_block, 'mp', axis=0, tiled=True)  230 us
    all_gather x11, waiting for transfers between devices, step(): lax.all_gather(norm_block, 'mp', axis=0, tiled=True)  208 us
    reduce_scatter x11, waiting for transfers between devices, step(): lax.psum_scatter(partial_value.astype(jnp.bfloat16), 'mp', scatter_dimens...  132 us
    dynamic_update_slice x44, other arithmetic, put_block(): lax.dynamic_update_index_in_dim(buffer, jnp.where(valid, update, former),...  83.6 us
    reduce_scatter x1, waiting for transfers between devices, per_device(): lax.psum_scatter(query_grad.astype(jnp.bfloat16), 'dp', scatter_dimension...  45.7 us
    reduce_scatter x1, waiting for transfers between devices, per_device(): lax.psum_scatter(out_grad.astype(jnp.bfloat16), 'dp', scatter_dimension=0...  44.8 us
    dynamic_slice x22, local copies, waits for them, and re-layouts, put_block(): former = lax.dynamic_index_in_dim(buffer, place, 0, keepdims=False)  39 us
    dot_general x11, matrix products, step(): jnp.dot(grad_all, w_o, preferred_element_type=f32)  33 us
  transfers between devices with their start and end apart: 49, of which 38 were waited for; matrix products, arithmetic and copies ran while one was open for 18% of the time, Pallas kernels for 0%

commit v1 on v0

v1 whole, which is shorter than its diff:
```python
import math

import jax
import jax.numpy as jnp
from jax import lax
from jax.sharding import PartitionSpec as P

HEAD_DIM = 64
LATENTS = 64
MICRO = 4


def shifted(x, axis, by):
    length = lax.axis_size(axis)
    pairs = [(i, i + by) for i in range(length) if 0 <= i + by < length]
    return lax.ppermute(x, axis, pairs)


def norm_forward(rows, gain, offset):
    mean = jnp.mean(rows, axis=-1, keepdims=True)
    centered = rows - mean
    rstd = lax.rsqrt(jnp.mean(centered * centered, axis=-1, keepdims=True) + 1e-05)
    normed = centered * rstd
    return (normed * gain + offset, normed, rstd)


def norm_back(grad, normed, rstd, gain):
    scaled = grad * gain
    mean_one = jnp.mean(scaled, axis=-1, keepdims=True)
    mean_two = jnp.mean(scaled * normed, axis=-1, keepdims=True)
    return (scaled - mean_one - normed * mean_two) * rstd


def from_ahead(x, axis, by):
    length = lax.axis_size(axis)
    pairs = [((i + by) % length, i) for i in range(length)]
    return lax.ppermute(x, axis, pairs)


def ring_pieces(x, axis):
    return [x] + [from_ahead(x, axis, by) for by in range(1, lax.axis_size(axis))]


def relay(grad_rows, input_rows, gain, gate, w_o, w_q, query_p, key_p, value_p, index_own):
    f32 = jnp.float32
    bf16 = jnp.bfloat16
    sections = lax.axis_size("section")
    section_at = lax.axis_index("section")
    rows, width = grad_rows.shape
    block = rows // MICRO
    n_vis = key_p[0].shape[0]
    ways = len(w_o)
    scale = 1.0 / math.sqrt(HEAD_DIM)
    image_of = jnp.arange(n_vis) // LATENTS
    first_step = sections - 1 - section_at
    last_section = section_at == sections - 1

    def split(x):
        return x.reshape(x.shape[0], -1, HEAD_DIM)

    allowed = image_of[None, :] == index_own[:, None]
    has_image = jnp.any(allowed, axis=1)
    probs, probs_b, attended = [], [], []
    for k in range(ways):
        scores = (
            jnp.einsum("thd,nhd->htn", split(query_p[k]), split(key_p[k]), preferred_element_type=f32)
            * scale
        )
        top = jnp.max(jnp.where(allowed[None], scores, -1e30), axis=2, keepdims=True)
        top = jnp.where(has_image[None, :, None], top, 0.0)
        expd = jnp.exp(jnp.where(allowed[None], scores - top, -jnp.inf))
        total = jnp.sum(expd, axis=2, keepdims=True) + (1.0 - has_image.astype(f32))[None, :, None]
        probs.append(expd / total)
        probs_b.append(probs[k].astype(bf16))
        attended.append(
            jnp.einsum("htn,nhd->thd", probs_b[k], split(value_p[k]), preferred_element_type=f32)
            .astype(bf16)
        )
    x32 = input_rows.astype(f32)
    mean = jnp.mean(x32, axis=-1, keepdims=True)
    centered = x32 - mean
    rstd = lax.rsqrt(jnp.mean(centered * centered, axis=-1, keepdims=True) + 1e-05)

    sent = jnp.zeros((block, width), bf16)
    dys, dxs, gas, gss, gqs = [], [], [], [], []
    for turn in range(MICRO + sections - 1):
        received = shifted(sent, "section", -1)
        start = jnp.clip(turn - first_step, 0, MICRO - 1) * block

        def cut(x, axis=0):
            return lax.dynamic_slice_in_dim(x, start, block, axis)

        dy = jnp.where(last_section, cut(grad_rows), received)
        ga, gs, gq = [], [], []
        grad_norm = jnp.zeros((block, width), f32)
        for k in range(ways):
            ga_k = (gate * jnp.dot(dy, w_o[k], preferred_element_type=f32)).astype(bf16)
            ga3 = split(ga_k)
            grad_probs = jnp.einsum("thd,nhd->htn", ga3, split(value_p[k]), preferred_element_type=f32)
            inner = jnp.einsum(
                "thd,thd->ht", ga3.astype(f32), cut(attended[k]).astype(f32)
            )
            gs_k = (cut(probs[k], 1) * (grad_probs - inner[:, :, None]) * scale).astype(bf16)
            gq_k = (
                jnp.einsum("htn,nhd->thd", gs_k, split(key_p[k]), preferred_element_type=f32)
                .astype(bf16)
                .reshape(block, -1)
            )
            grad_norm = grad_norm + lax.dot_general(
                gq_k, w_q[k], (((1,), (1,)), ((), ())), preferred_element_type=f32
            )
            ga.append(ga_k)
            gs.append(gs_k)
            gq.append(gq_k)
        rstd_b = cut(rstd)
        normed = (cut(input_rows).astype(f32) - cut(mean)) * rstd_b
        sent = (dy.astype(f32) + norm_back(grad_norm, normed, rstd_b, gain)).astype(bf16)
        dys.append(dy)
        dxs.append(sent)
        gas.append(ga)
        gss.append(gs)
        gqs.append(gq)

    def own(parts, axis=0):
        return lax.dynamic_slice_in_dim(
            jnp.concatenate(parts, axis), first_step * block, rows, axis
        )

    dy_all, dx_all = own(dys), own(dxs)
    gq_all, gk, gv, att = [], [], [], []
    for k in range(ways):
        ga_k = own([g[k] for g in gas])
        gs_k = own([g[k] for g in gss], 1)
        gq_all.append(own([g[k] for g in gqs]))
        gk.append(
            jnp.einsum("htn,thd->nhd", gs_k, split(query_p[k]), preferred_element_type=f32)
            .reshape(n_vis, -1)
        )
        gv.append(
            jnp.einsum("htn,thd->nhd", probs_b[k], split(ga_k), preferred_element_type=f32)
            .reshape(n_vis, -1)
        )
        att.append(attended[k].reshape(rows, -1))
    return dy_all, dx_all, gq_all, att, gk, gv


def per_device(
    upstream_grad,
    x_in,
    ln_gain,
    ln_bias,
    gate_alpha,
    w_query,
    w_key,
    w_value,
    w_out,
    queries,
    keys,
    values,
    image_index,
    latents,
    res_gain,
    res_bias,
):
    f32 = jnp.float32
    bf16 = jnp.bfloat16
    section_at = lax.axis_index("section")
    ways = lax.axis_size("mp")
    way_at = lax.axis_index("mp")
    rows, width = upstream_grad.shape[1:]
    gate = jnp.tanh(gate_alpha[0])
    gain, offset = ln_gain[0], ln_bias[0]
    grad_rows = upstream_grad[0]
    input_rows = x_in[0, 0]
    w_o = ring_pieces(w_out[0], "mp")
    w_q = ring_pieces(w_query[0], "mp")
    key_p = ring_pieces(keys[0, 0], "mp")
    value_p = ring_pieces(values[0, 0], "mp")
    query_p = []
    for k in range(ways):
        to = (way_at - k + ways) % ways
        piece = lax.dynamic_slice_in_dim(queries[0, 0], to * rows, rows, 0)
        query_p.append(from_ahead(piece, "mp", k) if k else piece)
    index_own = lax.dynamic_slice_in_dim(image_index[0], way_at * rows, rows, 0)
    dy_all, dx_all, gq, att, gk, gv = relay(
        grad_rows, input_rows, gain, gate, w_o, w_q, query_p, key_p, value_p, index_own
    )
    norm_rows = norm_forward(input_rows.astype(f32), gain, offset)[0].astype(bf16)
    contract_rows = (((0,), (0,)), ((), ()))

    def homed(parts, kind):
        total = parts[0].astype(f32)
        for k in range(1, ways):
            total = total + from_ahead(parts[k].astype(kind), "mp", -k).astype(f32)
        return total

    def over_rows(left, right):
        return lax.dot_general(left, right, contract_rows, preferred_element_type=f32)

    def scattered(x):
        return lax.psum_scatter(x.astype(bf16), "dp", scatter_dimension=0, tiled=True)

    key_b = homed(gk, f32).astype(bf16)
    value_b = homed(gv, f32).astype(bf16)
    out_grad = scattered(homed([gate * over_rows(dy_all, a) for a in att], bf16))
    query_grad = scattered(homed([over_rows(norm_rows, g) for g in gq], bf16))
    visual32, lat_normed, lat_rstd = norm_forward(latents.astype(f32), res_gain, res_bias)
    visual = visual32.astype(bf16)[0]
    both = scattered(
        over_rows(visual, jnp.concatenate([key_b, value_b], 1))
    )
    visual_part = (
        jnp.einsum("ni,ci->nc", key_b, w_key[0], preferred_element_type=f32)
        + jnp.einsum("ni,ci->nc", value_b, w_value[0], preferred_element_type=f32)
    )[None]
    visual_sum = lax.psum_scatter(visual_part, ("section", "mp"), scatter_dimension=1, tiled=True)
    share = visual_sum.shape[1]
    own_start = (section_at * ways + way_at) * share
    own_normed = lax.dynamic_slice_in_dim(lat_normed, own_start, share, 1)
    own_rstd = lax.dynamic_slice_in_dim(lat_rstd, own_start, share, 1)
    latent_grads = norm_back(visual_sum, own_normed, own_rstd, res_gain)
    inner = w_query.shape[2]
    return (
        dx_all[None, None],
        query_grad[None],
        both[:, :inner][None],
        both[:, inner:][None],
        out_grad[None],
        latent_grads,
    )


def solution(mesh):
    in_specs = (
        P("dp", "mp", None),
        P("section", "dp", "mp", None),
        P("section", None),
        P("section", None),
        P("section"),
        P("section", None, "mp"),
        P("section", None, "mp"),
        P("section", None, "mp"),
        P("section", None, "mp"),
        P("section", "dp", None, "mp"),
        P("section", "dp", None, "mp"),
        P("section", "dp", None, "mp"),
        P("dp", None),
        P("dp", None, None),
        P(),
        P(),
    )
    out_specs = (
        P("section", "dp", "mp", None),
        P("section", "dp", "mp"),
        P("section", "dp", "mp"),
        P("section", "dp", "mp"),
        P("section", "dp", "mp"),
        P("dp", ("section", "mp"), None),
    )
    return jax.shard_map(
        per_device, mesh=mesh, in_specs=in_specs, out_specs=out_specs, check_vma=False
    )
```

time: 1220 us -> 551 us (0.45)
  waiting for transfers between devices: 722 us -> 268 us
  other arithmetic: 203 us -> 57.6 us
  local copies, waits for them, and re-layouts: 116 us -> 47 us
    all_gather x22 -> x0, waiting for transfers between devices: 438 us -> none  [the longest x11 230 us: step(): lax.all_gather(grad_block, 'mp', axis=0, tiled=True)]
    reduce_scatter x15 -> x3, waiting for transfers between devices: 267 us -> 38.3 us  [scattered(): lax.psum_scatter(x.astype(bf16), 'dp', scatter_dimension=0, tiled=True)]
    ppermute x0 -> x9, waiting for transfers between devices: none -> 153 us  [from_ahead(): return lax.ppermute(x, axis, pairs)]
    dynamic_update_slice x44 -> x0, other arithmetic: 83.6 us -> none  [put_block(): lax.dynamic_update_index_in_dim(buffer, jnp.where(valid, update, former),...]
    ppermute x11 -> x7, waiting for transfers between devices: 0.03 us -> 76.5 us  [shifted(): return lax.ppermute(x, axis, pairs)]
    dynamic_slice x44 -> x7, local copies, waits for them, and re-layouts: 49.1 us -> 2.38 us  [the longest x2 2.06 us: per_device(): piece = lax.dynamic_slice_in_dim(queries[0, 0], to * rows, rows, 0)]
    while x484 -> x0, local copies, waits for them, and re-layouts: 29 us -> none
    reduce_sum x12 -> x1, other arithmetic: 29.3 us -> 1.12 us  [norm_back(): mean_one = jnp.mean(scaled, axis=-1, keepdims=True)]
  transfers between devices with their start and end apart: 49 -> 20, of which waited for: 38 -> 12; matrix products, arithmetic and copies ran while one was open for 18% -> 16% of each run, Pallas kernels for 0% -> 0%
where the time goes in v1:
time: 551 us; the launch traced here: 540 us
  waiting for transfers between devices  268 us (49%)
  matrix products  130 us (24%)
  other arithmetic  57.6 us (10%)
  local copies, waits for them, and re-layouts  47 us (9%)
  starting transfers between devices  21.5 us (4%)
  between operations  16.6 us (3%)
    ppermute x9, waiting for transfers between devices, from_ahead(): return lax.ppermute(x, axis, pairs)  153 us
    ppermute x7, waiting for transfers between devices, shifted(): return lax.ppermute(x, axis, pairs)  76.5 us
    reduce_scatter x3, waiting for transfers between devices, scattered(): lax.psum_scatter(x.astype(bf16), 'dp', scatter_dimension=0, tiled=True)  38.3 us
    dot_general x14, matrix products, relay(): jnp.einsum('thd,nhd->htn', ga3, split(value_p[k]), preferred_element_type...  30.8 us
    dot_general x14, matrix products, relay(): ga_k = (gate * jnp.dot(dy, w_o[k], preferred_element_type=f32)).astype(bf16)  27 us
    unnamed x12, other arithmetic  26.9 us
    dot_general x14, matrix products, relay(): lax.dot_general(gq_k, w_q[k], (((1,), (1,)), ((), ())), preferred_element...  25.6 us
    dot_general x5, matrix products, over_rows(): lax.dot_general(left, right, contract_rows, preferred_element_type=f32)  21.3 us
  transfers between devices with their start and end apart: 20, of which 12 were waited for; matrix products, arithmetic and copies ran while one was open for 16% of the time, Pallas kernels for 0%

profile of v1, /device:TPU:0, one launch (start us, length us, event | category | flops | bytes accessed | tf_op | source)
XLA Modules:
  0.0 540.4 jit_solution(108024065469715885)
XLA Ops:
  9.2 2.9 collective-permute-start.1
  17.9 3.0 convert_reduce_fusion
  33.9 3.0 select_reduce_fusion
  41.7 2.9 constant_dynamic-update-slice_fusion.54
  46.9 24.7 %collective-permute-done.3 = bf16[4096,256]{1,0:T(8,128)(2,1)} collective-permute-done((bf16[4096,256]{1,0:T(8,128)(2,1)S(1)}, bf16[4096,256]{1,0:T(8,128)(2,1)}, u32[]{:S(2)}, u32[]{:S(2)}) %collective-permute-start.3) | collective-permute-done | bytes 2097184 | tf_op jit(solution)/shard_map/ppermute | solution.py:37
  71.5 3.0 constant_dynamic-update-slice_fusion.47
  82.3 33.4 %collective-permute-done.5 = bf16[4096,256]{1,0:T(8,128)(2,1)} collective-permute-done((bf16[4096,256]{1,0:T(8,128)(2,1)}, bf16[4096,256]{1,0:T(8,128)(2,1)}, u32[]{:S(2)}, u32[]{:S(2)}) %collective-permute-start.5) | collective-permute-done | bytes 2097184 | tf_op jit(solution)/shard_map/ppermute | solution.py:37
  115.7 2.8 fusion.201
  122.1 2.8 collective-permute-done.6
  143.6 2.8 fusion.200
  149.7 14.5 %collective-permute-done.7 = bf16[128,4096]{1,0:T(8,128)(2,1)S(1)} collective-permute-done((bf16[128,4096]{1,0:T(8,128)(2,1)S(1)}, bf16[128,4096]{1,0:T(8,128)(2,1)S(1)}, u32[]{:S(2)}, u32[]{:S(2)}) %collective-permute-start.7) | collective-permute-done | bytes 1048608 | tf_op jit(solution)/shard_map/ppermute | solution.py:16
  167.6 2.7 constant_dynamic-update-slice_fusion.45
  183.1 2.8 fusion.199
  189.3 14.6 %collective-permute-done.8 = bf16[128,4096]{1,0:T(8,128)(2,1)S(1)} collective-permute-done((bf16[128,4096]{1,0:T(8,128)(2,1)S(1)}, bf16[128,4096]{1,0:T(8,128)(2,1)S(1)}, u32[]{:S(2)}, u32[]{:S(2)}) %collective-permute-start.8) | collective-permute-done | bytes 1048608 | tf_op jit(solution)/shard_map/ppermute | solution.py:16
  222.8 2.8 fusion.198
  228.8 14.8 %collective-permute-done.9 = bf16[128,4096]{1,0:T(8,128)(2,1)S(1)} collective-permute-done((bf16[128,4096]{1,0:T(8,128)(2,1)S(1)}, bf16[128,4096]{1,0:T(8,128)(2,1)S(1)}, u32[]{:S(2)}, u32[]{:S(2)}) %collective-permute-start.9) | collective-permute-done | bytes 1048608 | tf_op jit(solution)/shard_map/ppermute | solution.py:16
  262.5 2.8 fusion.197
  268.8 14.6 %collective-permute-done.10 = bf16[128,4096]{1,0:T(8,128)(2,1)S(1)} collective-permute-done((bf16[128,4096]{1,0:T(8,128)(2,1)S(1)}, bf16[128,4096]{1,0:T(8,128)(2,1)S(1)}, u32[]{:S(2)}, u32[]{:S(2)}) %collective-permute-start.10) | collective-permute-done | bytes 1048608 | tf_op jit(solution)/shard_map/ppermute | solution.py:16
  302.1 2.8 fusion.196
  308.6 15.2 %collective-permute-done.11 = bf16[128,4096]{1,0:T(8,128)(2,1)} collective-permute-done((bf16[128,4096]{1,0:T(8,128)(2,1)}, bf16[128,4096]{1,0:T(8,128)(2,1)}, u32[]{:S(2)}, u32[]{:S(2)}) %collective-permute-start.11) | collective-permute-done | bytes 1048608 | tf_op jit(solution)/shard_map/ppermute | solution.py:16
  323.8 2.8 constant_dynamic-update-slice_fusion.48
  327.5 2.7 constant_dynamic-update-slice_fusion.41
  352.1 8.4 %collective-permute-done.14 = f32[320,256]{0,1:T(8,128)S(1)} collective-permute-done((f32[320,256]{0,1:T(8,128)S(1)}, f32[320,256]{0,1:T(8,128)S(1)}, u32[]{:S(2)}, u32[]{:S(2)}) %collective-permute-start.14) | collective-permute-done | bytes 327712 | tf_op jit(solution)/shard_map/ppermute | solution.py:37
  364.5 4.8 fusion.9
  372.6 44.7 %collective-permute-done.15 = bf16[4096,256]{1,0:T(8,128)(2,1)} collective-permute-done((bf16[4096,256]{1,0:T(8,128)(2,1)}, bf16[4096,256]{1,0:T(8,128)(2,1)}, u32[]{:S(2)}, u32[]{:S(2)}) %collective-permute-start.15) | collective-permute-done | bytes 2097184 | tf_op jit(solution)/shard_map/ppermute | solution.py:37
  417.4 5.5 %fusion.8 = bf16[4096,256]{1,0:T(8,128)(2,1)} fusion(bf16[512,256]{0,1:T(8,128)(2,1)S(1)} %bitcast.494, bf16[4096,256]{1,0:T(8,128)(2,1)} %collective-permute-done.15, bf16[896,4096]{1,0:T(8,128)(2,1)} %get-tuple-element.26, s32[]{:T(128)S(6)} %select_n.202, f32[]{:T(128)} %bitcast.32), kind=kOutput, calls=%fused_computation.12 | convolution fusion | flops 1077936128 | bytes 8651268 | tf_op jit(solution)/shard_map/dot_general | solution.py:198
  424.4 4.9 convolution_convert_fusion
  431.0 41.6 %collective-permute-done.12 = bf16[4096,256]{1,0:T(8,128)(2,1)S(1)} collective-permute-done((bf16[4096,256]{1,0:T(8,128)(2,1)S(1)}, bf16[4096,256]{1,0:T(8,128)(2,1)S(1)}, u32[]{:S(2)}, u32[]{:S(2)}) %collective-permute-start.12) | collective-permute-done | bytes 2097184 | tf_op jit(solution)/shard_map/ppermute | solution.py:37
  472.5 4.1 add_convert_fusion
  481.0 2.9 fusion.195
  485.8 4.7 dynamic-slice_bitcast_fusion
  495.1 38.3 %reduce-scatter.5.cloned.1.call-done = bf16[1024,256]{1,0:T(8,128)(2,1)} async-done(((bf16[4096,256]{1,0:T(8,128)(2,1)}), bf16[1024,256]{1,0:T(8,128)(2,1)}) %reduce-scatter.5.cloned.1.call-update) | async-done | bytes 524304 | tf_op jit(solution)/shard_map/reduce_scatter | solution.py:201
  (403 shorter events, 189.2 us)
Async XLA Ops:
  7.2 353.4 %copy-start = (bf16[1,1024,256]{2,1,0:T(8,128)(2,1)S(1)}, bf16[1,1024,256]{2,1,0:T(8,128)(2,1)}, u32[]{:S(2)}) copy-start(bf16[1,1024,256]{2,1,0:T(8,128)(2,1)} %param.23) | copy-start | bytes 1572868
  7.2 9.4 %copy-start.10 = (bf16[1,4096,256]{2,1,0:T(8,128)(2,1)S(1)}, bf16[1,4096,256]{2,1,0:T(8,128)(2,1)}, u32[]{:S(2)}) copy-start(bf16[1,4096,256]{2,1,0:T(8,128)(2,1)} %param.24) | copy-start | bytes 6291460
  7.2 483.4 %reduce-scatter.11.cloned.1.call-start = ((), (), s32[]{:S(2)}) async-start(), calls=%async_computation.7 | async-start | bytes 1474560 | tf_op jit(solution)/shard_map/reduce_scatter | solution.py:216
  9.2 22.9 %collective-permute-start.1 = (bf16[512,256]{1,0:T(8,128)(2,1)}, bf16[512,256]{1,0:T(8,128)(2,1)}, u32[]{:S(2)}, u32[]{:S(2)}) collective-permute-start(bf16[512,256]{1,0:T(8,128)(2,1)} %get-tuple-element.52), channel_id=1, source_target_pairs={{4,0},{0,4},{5,1},{1,5},{6,2},{2,6},{7,3},{3,7},{12,8},{8,12},{13,... | collective-permute-start | bytes 786440 | tf_op jit(solution)/shard_map/ppermute | solution.py:37
  12.1 15.1 %collective-permute-start.2 = (bf16[320,256]{1,0:T(8,128)(2,1)}, bf16[320,256]{1,0:T(8,128)(2,1)S(1)}, u32[]{:S(2)}, u32[]{:S(2)}) collective-permute-start(bf16[320,256]{1,0:T(8,128)(2,1)} %bitcast.550), channel_id=1, source_target_pairs={{4,0},{0,4},{5,1},{1,5},{6,2},{2,6},{7,3},{3,7},{12,8},{8,12},{13,... | collective-permute-start | bytes 491528 | tf_op jit(solution)/shard_map/ppermute | solution.py:37
  12.2 18.8 %collective-permute-start.4 = (bf16[320,256]{1,0:T(8,128)(2,1)}, bf16[320,256]{1,0:T(8,128)(2,1)}, u32[]{:S(2)}, u32[]{:S(2)}) collective-permute-start(bf16[320,256]{1,0:T(8,128)(2,1)} %bitcast.551), channel_id=1, source_target_pairs={{4,0},{0,4},{5,1},{1,5},{6,2},{2,6},{7,3},{3,7},{12,8},{8,12},{13,... | collective-permute-start | bytes 491528 | tf_op jit(solution)/shard_map/ppermute | solution.py:37
  15.3 26.5 %collective-permute-start = (bf16[128,4096]{1,0:T(8,128)(2,1)}, bf16[128,4096]{1,0:T(8,128)(2,1)}, u32[]{:S(2)}, u32[]{:S(2)}) collective-permute-start(bf16[128,4096]{1,0:T(8,128)(2,1)} %broadcast_in_dim.56), channel_id=1, source_target_pairs={{8,0},{16,8},{24,16},{9,1},{17,9},{25,17},{10,2},{18,10},{26,18},{... | collective-permute-start | bytes 3145736 | tf_op jit(solution)/shard_map/ppermute | solution.py:16
  16.6 55.0 %collective-permute-start.3 = (bf16[4096,256]{1,0:T(8,128)(2,1)S(1)}, bf16[4096,256]{1,0:T(8,128)(2,1)}, u32[]{:S(2)}, u32[]{:S(2)}) collective-permute-start(bf16[4096,256]{1,0:T(8,128)(2,1)S(1)} %bitcast.456), channel_id=1, source_target_pairs={{4,0},{0,4},{5,1},{1,5},{6,2},{2,6},{7,3},{3,7},{12,8},{8,12},{13,... | collective-permute-start | bytes 6291464 | tf_op jit(solution)/shard_map/ppermute | solution.py:37
  27.9 87.7 %collective-permute-start.5 = (bf16[4096,256]{1,0:T(8,128)(2,1)}, bf16[4096,256]{1,0:T(8,128)(2,1)}, u32[]{:S(2)}, u32[]{:S(2)}) collective-permute-start(bf16[4096,256]{1,0:T(8,128)(2,1)} %bitcast.457), channel_id=1, source_target_pairs={{4,0},{0,4},{5,1},{1,5},{6,2},{2,6},{7,3},{3,7},{12,8},{8,12},{13,... | collective-permute-start | bytes 6291464 | tf_op jit(solution)/shard_map/ppermute | solution.py:37
  79.0 36.7 %copy-start.52 = (bf16[4,128,64]{1,2,0:T(8,128)(2,1)}, bf16[4,128,64]{1,2,0:T(8,128)(2,1)S(1)}, u32[]{:S(2)}) copy-start(bf16[4,128,64]{1,2,0:T(8,128)(2,1)S(1)} %convolution_convert_fusion.16) | copy-start | bytes 196612
  81.4 34.3 %copy-start.2 = (bf16[1,1,512,4096]{3,2,1,0:T(8,128)(2,1)S(1)}, bf16[1,1,512,4096]{3,2,1,0:T(8,128)(2,1)}, u32[]{:S(2)}) copy-start(bf16[1,1,512,4096]{3,2,1,0:T(8,128)(2,1)} %param.17) | copy-start | bytes 12582916
  81.4 34.2 %copy-start.51 = (f32[1,4096]{1,0:T(1,128)S(1)}, f32[1,4096]{1,0:T(1,128)}, u32[]{:S(2)}) copy-start(f32[1,4096]{1,0:T(1,128)} %param.18) | copy-start | bytes 49156
  81.4 34.2 %copy-start.101 = (f32[128]{0:T(128)S(1)}, f32[128]{0:T(128)}, u32[]{:S(2)}) copy-start(f32[128]{0:T(128)} %get-tuple-element.66) | copy-start | bytes 1540
  81.4 34.2 %copy-start.102 = (f32[128]{0:T(128)S(1)}, f32[128]{0:T(128)}, u32[]{:S(2)}) copy-start(f32[128]{0:T(128)} %get-tuple-element.142) | copy-start | bytes 1540
  120.4 4.5 collective-permute-start.6
  148.5 15.8 %collective-permute-start.7 = (bf16[128,4096]{1,0:T(8,128)(2,1)S(1)}, bf16[128,4096]{1,0:T(8,128)(2,1)S(1)}, u32[]{:S(2)}, u32[]{:S(2)}) collective-permute-start(bf16[128,4096]{1,0:T(8,128)(2,1)S(1)} %get-tuple-element.49), channel_id=1, source_target_pairs={{8,0},{16,8},{24,16},{9,1},{17,9},{25,17},{10,2},{18,10},{26,18},{... | collective-permute-start | bytes 3145736 | tf_op jit(solution)/shard_map/ppermute | solution.py:16
  187.9 16.1 %collective-permute-start.8 = (bf16[128,4096]{1,0:T(8,128)(2,1)S(1)}, bf16[128,4096]{1,0:T(8,128)(2,1)S(1)}, u32[]{:S(2)}, u32[]{:S(2)}) collective-permute-start(bf16[128,4096]{1,0:T(8,128)(2,1)S(1)} %get-tuple-element.47), channel_id=1, source_target_pairs={{8,0},{16,8},{24,16},{9,1},{17,9},{25,17},{10,2},{18,10},{26,18},{... | collective-permute-start | bytes 3145736 | tf_op jit(solution)/shard_map/ppermute | solution.py:16
  227.5 16.1 %collective-permute-start.9 = (bf16[128,4096]{1,0:T(8,128)(2,1)S(1)}, bf16[128,4096]{1,0:T(8,128)(2,1)S(1)}, u32[]{:S(2)}, u32[]{:S(2)}) collective-permute-start(bf16[128,4096]{1,0:T(8,128)(2,1)S(1)} %get-tuple-element.45), channel_id=1, source_target_pairs={{8,0},{16,8},{24,16},{9,1},{17,9},{25,17},{10,2},{18,10},{26,18},{... | collective-permute-start | bytes 3145736 | tf_op jit(solution)/shard_map/ppermute | solution.py:16
  267.3 16.1 %collective-permute-start.10 = (bf16[128,4096]{1,0:T(8,128)(2,1)S(1)}, bf16[128,4096]{1,0:T(8,128)(2,1)S(1)}, u32[]{:S(2)}, u32[]{:S(2)}) collective-permute-start(bf16[128,4096]{1,0:T(8,128)(2,1)S(1)} %get-tuple-element.43), channel_id=1, source_target_pairs={{8,0},{16,8},{24,16},{9,1},{17,9},{25,17},{10,2},{18,10},{26,18},{... | collective-permute-start | bytes 3145736 | tf_op jit(solution)/shard_map/ppermute | solution.py:16
  307.3 16.5 %collective-permute-start.11 = (bf16[128,4096]{1,0:T(8,128)(2,1)}, bf16[128,4096]{1,0:T(8,128)(2,1)}, u32[]{:S(2)}, u32[]{:S(2)}) collective-permute-start(bf16[128,4096]{1,0:T(8,128)(2,1)} %get-tuple-element.41), channel_id=1, source_target_pairs={{8,0},{16,8},{24,16},{9,1},{17,9},{25,17},{10,2},{18,10},{26,18},{... | collective-permute-start | bytes 3145736 | tf_op jit(solution)/shard_map/ppermute | solution.py:16
  331.2 7.5 %copy-start.22 = (bf16[128,4096]{1,0:T(8,128)(2,1)S(1)}, bf16[128,4096]{1,0:T(8,128)(2,1)}, u32[]{:S(2)}) copy-start(bf16[128,4096]{1,0:T(8,128)(2,1)} %copy-done.21) | copy-start | bytes 3145732
  337.2 23.7 %collective-permute-start.13 = (f32[320,256]{0,1:T(8,128)}, f32[320,256]{0,1:T(8,128)}, u32[]{:S(2)}, u32[]{:S(2)}) collective-permute-start(f32[320,256]{0,1:T(8,128)} %bitcast.176), channel_id=1, source_target_pairs={{4,0},{0,4},{5,1},{1,5},{6,2},{2,6},{7,3},{3,7},{12,8},{8,12},{13,... | collective-permute-start | bytes 983048 | tf_op jit(solution)/shard_map/ppermute | solution.py:37
  349.0 11.5 %collective-permute-start.14 = (f32[320,256]{0,1:T(8,128)S(1)}, f32[320,256]{0,1:T(8,128)S(1)}, u32[]{:S(2)}, u32[]{:S(2)}) collective-permute-start(f32[320,256]{0,1:T(8,128)S(1)} %bitcast.549), channel_id=1, source_target_pairs={{4,0},{0,4},{5,1},{1,5},{6,2},{2,6},{7,3},{3,7},{12,8},{8,12},{13,... | collective-permute-start | bytes 983048 | tf_op jit(solution)/shard_map/ppermute | solution.py:37
  352.0 8.9 %copy-start.48 = (f32[4,64,320]{2,1,0:T(8,128)S(1)}, f32[4,64,320]{2,1,0:T(8,128)}, u32[]{:S(2)}) copy-start(f32[4,64,320]{2,1,0:T(8,128)} %fusion.85) | copy-start | bytes 983044
  352.0 10.0 %copy-start.74 = (bf16[1,1024,256]{2,1,0:T(8,128)(2,1)S(1)}, bf16[1,1024,256]{2,1,0:T(8,128)(2,1)}, u32[]{:S(2)}) copy-start(bf16[1,1024,256]{2,1,0:T(8,128)(2,1)} %param.22) | copy-start | bytes 1572868
  363.6 129.9 %reduce-scatter.7.cloned.1.call-start = ((), (), s32[]{:S(2)}) async-start(), calls=%async_computation.5 | async-start | bytes 1310720 | tf_op jit(solution)/shard_map/reduce_scatter | solution.py:201
  369.4 48.0 %collective-permute-start.15 = (bf16[4096,256]{1,0:T(8,128)(2,1)}, bf16[4096,256]{1,0:T(8,128)(2,1)}, u32[]{:S(2)}, u32[]{:S(2)}) collective-permute-start(bf16[4096,256]{1,0:T(8,128)(2,1)} %fusion.9), channel_id=1, source_target_pairs={{4,0},{0,4},{5,1},{1,5},{6,2},{2,6},{7,3},{3,7},{12,8},{8,12},{13,... | collective-permute-start | bytes 6291464 | tf_op jit(solution)/shard_map/ppermute | solution.py:37
  370.3 47.1 %copy-start.46 = (bf16[4,512,64]{1,2,0:T(8,128)(2,1)S(1)}, bf16[4,512,64]{1,2,0:T(8,128)(2,1)}, u32[]{:S(2)}) copy-start(bf16[4,512,64]{1,2,0:T(8,128)(2,1)} %convolution_convert_fusion.3) | copy-start | bytes 786436
  372.3 122.8 %reduce-scatter.9.cloned.1.call-start = ((), (), s32[]{:S(2)}) async-start(), calls=%async_computation.6 | async-start | bytes 2621440 | tf_op jit(solution)/shard_map/reduce_scatter | solution.py:201
  423.0 110.5 %reduce-scatter.5.cloned.1.call-start = ((), (), s32[]{:S(2)}) async-start(), calls=%async_computation.4 | async-start | bytes 2621440 | tf_op jit(solution)/shard_map/reduce_scatter | solution.py:201
  424.3 48.2 %copy-start.8 = (bf16[1,1,512,4096]{3,2,1,0:T(8,128)(2,1)S(1)}, bf16[1,1,512,4096]{3,2,1,0:T(8,128)(2,1)}, u32[]{:S(2)}) copy-start(bf16[1,1,512,4096]{3,2,1,0:T(8,128)(2,1)} %param.17) | copy-start | bytes 12582916
  429.3 43.3 %collective-permute-start.12 = (bf16[4096,256]{1,0:T(8,128)(2,1)S(1)}, bf16[4096,256]{1,0:T(8,128)(2,1)S(1)}, u32[]{:S(2)}, u32[]{:S(2)}) collective-permute-start(bf16[4096,256]{1,0:T(8,128)(2,1)S(1)} %convolution_convert_fusion), channel_id=1, source_target_pairs={{4,0},{0,4},{5,1},{1,5},{6,2},{2,6},{7,3},{3,7},{12,8},{8,12},{13,... | collective-permute-start | bytes 6291464 | tf_op jit(solution)/shard_map/ppermute | solution.py:37
  (94 other events, 259.7 us)
Sparse Core Ops, SparseCore 0:
  363.7 49.6 reduce-scatter.10
  415.7 26.2 reduce-scatter.6
  445.0 42.5 reduce-scatter.8
  490.2 43.1 reduce-scatter.4

commit v2 on v1

v2 whole, which is shorter than its diff:
```python
import functools
import math

import jax
import jax.numpy as jnp
from jax import lax
from jax.experimental import pallas as pl
from jax.experimental.pallas import tpu as pltpu
from jax.sharding import PartitionSpec as P

HEAD_DIM = 64
LATENTS = 64
MICRO = 4


def norm_forward(rows, gain, offset):
    mean = jnp.mean(rows, axis=-1, keepdims=True)
    centered = rows - mean
    rstd = lax.rsqrt(jnp.mean(centered * centered, axis=-1, keepdims=True) + 1e-05)
    normed = centered * rstd
    return (normed * gain + offset, normed, rstd)


def norm_back(grad, normed, rstd, gain):
    scaled = grad * gain
    mean_one = jnp.mean(scaled, axis=-1, keepdims=True)
    mean_two = jnp.mean(scaled * normed, axis=-1, keepdims=True)
    return (scaled - mean_one - normed * mean_two) * rstd


def from_ahead(x, axis, by):
    length = lax.axis_size(axis)
    pairs = [((i + by) % length, i) for i in range(length)]
    return lax.ppermute(x, axis, pairs)


def ring_pieces(x, axis):
    return [x] + [from_ahead(x, axis, by) for by in range(1, lax.axis_size(axis))]


def relay_kernel(
    sections,
    gate_ref,
    gain_ref,
    mean_ref,
    rstd_ref,
    probs_ref,
    att_ref,
    query_t_ref,
    key_ref,
    value_ref,
    x_ref,
    w_o_ref,
    w_q_ref,
    up_ref,
    dy_out,
    dx_out,
    gq_ref,
    gk_ref,
    gv_ref,
    dy_buf,
    dx_buf,
    back_buf,
    gs_buf,
    up_sem,
    send_sem,
    recv_sem,
    dy_sem,
    dx_sem,
):
    f32 = jnp.float32
    bf16 = jnp.bfloat16
    section_at = lax.axis_index("section")
    below = lax.rem(section_at + sections - 1, sections)
    above = lax.rem(section_at + 1, sections)
    heads, rows, n_vis = probs_ref.shape
    block = rows // MICRO
    width = x_ref.shape[1]
    inner = key_ref.shape[1]
    scale = 1.0 / math.sqrt(HEAD_DIM)
    is_last = section_at == sections - 1
    not_last = section_at < sections - 1
    not_first = section_at > 0

    def at(i):
        return pl.ds(pl.multiple_of(i * block, block), block)

    def load(i):
        return pltpu.make_async_copy(up_ref.at[at(i)], dy_buf.at[at(i)], up_sem.at[i])

    def hop(i):
        return pltpu.make_async_remote_copy(
            src_ref=dx_buf.at[at(i)],
            dst_ref=dy_buf.at[at(i)],
            send_sem=send_sem.at[i],
            recv_sem=recv_sem.at[i],
            device_id={"section": below},
            device_id_type=pl.DeviceIdType.MESH,
        )

    def dy_store(i):
        return pltpu.make_async_copy(dy_buf.at[at(i)], dy_out.at[at(i)], dy_sem.at[i])

    def dx_store(i):
        return pltpu.make_async_copy(dx_buf.at[at(i)], dx_out.at[at(i)], dx_sem.at[i])

    @pl.when(is_last)
    def _():
        for i in range(MICRO):
            load(i).start()

    barrier = pltpu.get_barrier_semaphore()
    for other in (below, above):
        pl.semaphore_signal(
            barrier, inc=1, device_id={"section": other}, device_id_type=pl.DeviceIdType.MESH
        )
    pl.semaphore_wait(barrier, 2)

    gk_ref[...] = jnp.zeros_like(gk_ref)
    gv_ref[...] = jnp.zeros_like(gv_ref)
    gate = gate_ref[0]
    nt = (((1,), (1,)), ((), ()))
    chunk = 512 if width % 512 == 0 else width
    few = 16

    def turn(i, carry):
        r = at(i)

        @pl.when(is_last)
        def _():
            load(i).wait()

        @pl.when(not_last)
        def _():
            hop(i).wait_recv()

        dy_store(i).start()
        ga32 = gate * jnp.dot(dy_buf[r, :], w_o_ref[...], preferred_element_type=f32)
        ga = ga32.astype(bf16)
        ga_r = ga.astype(f32)
        ga_t = ga32.T.astype(bf16)
        prod = ga_r * att_ref[r, :].astype(f32)
        gqs = []
        for h in range(heads):
            f = slice(h * HEAD_DIM, (h + 1) * HEAD_DIM)
            grad_probs = lax.dot_general(
                ga[:, f], value_ref[:, f], nt, preferred_element_type=f32
            )
            inner_sum = jnp.sum(prod[:, f], axis=1, keepdims=True)
            gs = (probs_ref[h, r, :].astype(f32) * (grad_probs - inner_sum) * scale).astype(bf16)
            gs_buf[h] = gs
            gqs.append(jnp.dot(gs, key_ref[:, f], preferred_element_type=f32))
        gq = jnp.concatenate(gqs, axis=1).astype(bf16)
        gq_ref[r, :] = gq

        def back(c, carry):
            cols = pl.ds(pl.multiple_of(c * chunk, chunk), chunk)
            back_buf[:, cols] = lax.dot_general(
                gq_ref[r, :], w_q_ref[cols, :], nt, preferred_element_type=f32
            )
            return carry

        lax.fori_loop(0, width // chunk, back, 0)

        def norm(c, carry):
            own = pl.ds(pl.multiple_of(c * few, few), few)
            far = pl.ds(pl.multiple_of(i * block + c * few, few), few)
            rstd = rstd_ref[far, :]
            normed = (x_ref[far, :].astype(f32) - mean_ref[far, :]) * rstd
            scaled = back_buf[own, :] * gain_ref[...]
            mean_one = jnp.sum(scaled, axis=1, keepdims=True) * (1.0 / width)
            mean_two = jnp.sum(scaled * normed, axis=1, keepdims=True) * (1.0 / width)
            add = (scaled - mean_one - normed * mean_two) * rstd
            dx_buf[far, :] = (dy_buf[far, :].astype(f32) + add).astype(bf16)
            return carry

        lax.fori_loop(0, block // few, norm, 0)

        @pl.when(not_first)
        def _():
            hop(i).start()

        dx_store(i).start()
        for h in range(heads):
            f = slice(h * HEAD_DIM, (h + 1) * HEAD_DIM)
            gk_ref[f, :] += jnp.dot(query_t_ref[i, f, :], gs_buf[h], preferred_element_type=f32)
            gv_ref[f, :] += jnp.dot(ga_t[f, :], probs_ref[h, r, :], preferred_element_type=f32)
        return carry

    lax.fori_loop(0, MICRO, turn, 0)
    for i in range(MICRO):
        dy_store(i).wait()
        dx_store(i).wait()

    @pl.when(not_first)
    def _():
        for i in range(MICRO):
            hop(i).wait_send()


def relay(grad_rows, input_rows, mean, rstd, gain, gate, w_o, w_q, query_p, key_p, value_p, index_own):
    f32 = jnp.float32
    bf16 = jnp.bfloat16
    sections = lax.axis_size("section")
    rows, width = grad_rows.shape
    block = rows // MICRO
    n_vis = key_p[0].shape[0]
    ways = len(w_o)
    scale = 1.0 / math.sqrt(HEAD_DIM)
    image_of = jnp.arange(n_vis) // LATENTS
    query = jnp.concatenate(query_p, 1)
    key = jnp.concatenate(key_p, 1)
    value = jnp.concatenate(value_p, 1)
    inner = query.shape[1]
    heads = inner // HEAD_DIM

    def split(x):
        return x.reshape(x.shape[0], -1, HEAD_DIM)

    allowed = image_of[None, :] == index_own[:, None]
    has_image = jnp.any(allowed, axis=1)
    scores = (
        jnp.einsum("thd,nhd->htn", split(query), split(key), preferred_element_type=f32) * scale
    )
    top = jnp.max(jnp.where(allowed[None], scores, -1e30), axis=2, keepdims=True)
    top = jnp.where(has_image[None, :, None], top, 0.0)
    expd = jnp.exp(jnp.where(allowed[None], scores - top, -jnp.inf))
    total = jnp.sum(expd, axis=2, keepdims=True) + (1.0 - has_image.astype(f32))[None, :, None]
    probs = (expd / total).astype(bf16)
    attended = (
        jnp.einsum("htn,nhd->thd", probs, split(value), preferred_element_type=f32)
        .astype(bf16)
        .reshape(rows, inner)
    )
    query_t = query.reshape(MICRO, block, inner).transpose(0, 2, 1)
    vmem = pl.BlockSpec(memory_space=pltpu.VMEM)
    hbm = pl.BlockSpec(memory_space=pl.ANY)
    shape = jax.ShapeDtypeStruct
    dy_all, dx_all, gq, gk_t, gv_t = pl.pallas_call(
        functools.partial(relay_kernel, sections),
        out_shape=(
            shape((rows, width), bf16),
            shape((rows, width), bf16),
            shape((rows, inner), bf16),
            shape((inner, n_vis), f32),
            shape((inner, n_vis), f32),
        ),
        in_specs=[pl.BlockSpec(memory_space=pltpu.SMEM)] + [vmem] * 11 + [hbm],
        out_specs=(hbm, hbm, vmem, vmem, vmem),
        scratch_shapes=[
            pltpu.VMEM((rows, width), bf16),
            pltpu.VMEM((rows, width), bf16),
            pltpu.VMEM((block, width), f32),
            pltpu.VMEM((heads, block, n_vis), bf16),
            pltpu.SemaphoreType.DMA((MICRO,)),
            pltpu.SemaphoreType.DMA((MICRO,)),
            pltpu.SemaphoreType.DMA((MICRO,)),
            pltpu.SemaphoreType.DMA((MICRO,)),
            pltpu.SemaphoreType.DMA((MICRO,)),
        ],
        compiler_params=pltpu.CompilerParams(
            collective_id=0, has_side_effects=True, vmem_limit_bytes=48 * 1024 * 1024
        ),
        cost_estimate=pl.CostEstimate(
            flops=4 * rows * width * inner + 8 * rows * n_vis * inner,
            bytes_accessed=2 * (4 * rows * width + 2 * width * inner),
            transcendentals=0,
        ),
        name="relay",
    )(
        gate.reshape(1),
        gain[None],
        mean,
        rstd,
        probs,
        attended,
        query_t,
        key,
        value,
        input_rows,
        jnp.concatenate(w_o, 1),
        jnp.concatenate(w_q, 1),
        grad_rows,
    )

    def parted(x, axis):
        return jnp.split(x, ways, axis)

    return dy_all, dx_all, parted(gq, 1), parted(attended, 1), parted(gk_t, 0), parted(gv_t, 0)


def per_device(
    upstream_grad,
    x_in,
    ln_gain,
    ln_bias,
    gate_alpha,
    w_query,
    w_key,
    w_value,
    w_out,
    queries,
    keys,
    values,
    image_index,
    latents,
    res_gain,
    res_bias,
):
    f32 = jnp.float32
    bf16 = jnp.bfloat16
    section_at = lax.axis_index("section")
    ways = lax.axis_size("mp")
    way_at = lax.axis_index("mp")
    rows, width = upstream_grad.shape[1:]
    gate = jnp.tanh(gate_alpha[0])
    gain, offset = ln_gain[0], ln_bias[0]
    grad_rows = upstream_grad[0]
    input_rows = x_in[0, 0]
    w_o = ring_pieces(w_out[0], "mp")
    w_q = ring_pieces(w_query[0], "mp")
    key_p = ring_pieces(keys[0, 0], "mp")
    value_p = ring_pieces(values[0, 0], "mp")
    query_p = []
    for k in range(ways):
        to = (way_at - k + ways) % ways
        piece = lax.dynamic_slice_in_dim(queries[0, 0], to * rows, rows, 0)
        query_p.append(from_ahead(piece, "mp", k) if k else piece)
    index_own = lax.dynamic_slice_in_dim(image_index[0], way_at * rows, rows, 0)
    x32 = input_rows.astype(f32)
    mean = jnp.mean(x32, axis=-1, keepdims=True)
    centered = x32 - mean
    rstd = lax.rsqrt(jnp.mean(centered * centered, axis=-1, keepdims=True) + 1e-05)
    norm_rows = (centered * rstd * gain + offset).astype(bf16)
    dy_all, dx_all, gq, att, gk, gv = relay(
        grad_rows, input_rows, mean, rstd, gain, gate, w_o, w_q, query_p, key_p, value_p, index_own
    )
    contract_rows = (((0,), (0,)), ((), ()))

    def homed(parts, kind):
        total = parts[0].astype(f32)
        for k in range(1, ways):
            total = total + from_ahead(parts[k].astype(kind), "mp", -k).astype(f32)
        return total

    def over_rows(left, right):
        return lax.dot_general(left, right, contract_rows, preferred_element_type=f32)

    def scattered(x):
        return lax.psum_scatter(x.astype(bf16), "dp", scatter_dimension=0, tiled=True)

    key_b = homed(gk, f32).T.astype(bf16)
    value_b = homed(gv, f32).T.astype(bf16)
    out_grad = scattered(homed([gate * over_rows(dy_all, a) for a in att], bf16))
    query_grad = scattered(homed([over_rows(norm_rows, g) for g in gq], bf16))
    visual32, lat_normed, lat_rstd = norm_forward(latents.astype(f32), res_gain, res_bias)
    visual = visual32.astype(bf16)[0]
    both = scattered(
        over_rows(visual, jnp.concatenate([key_b, value_b], 1))
    )
    visual_part = (
        jnp.einsum("ni,ci->nc", key_b, w_key[0], preferred_element_type=f32)
        + jnp.einsum("ni,ci->nc", value_b, w_value[0], preferred_element_type=f32)
    )[None]
    visual_sum = lax.psum_scatter(visual_part, ("section", "mp"), scatter_dimension=1, tiled=True)
    share = visual_sum.shape[1]
    own_start = (section_at * ways + way_at) * share
    own_normed = lax.dynamic_slice_in_dim(lat_normed, own_start, share, 1)
    own_rstd = lax.dynamic_slice_in_dim(lat_rstd, own_start, share, 1)
    latent_grads = norm_back(visual_sum, own_normed, own_rstd, res_gain)
    inner = w_query.shape[2]
    return (
        dx_all[None, None],
        query_grad[None],
        both[:, :inner][None],
        both[:, inner:][None],
        out_grad[None],
        latent_grads,
    )


def solution(mesh):
    in_specs = (
        P("dp", "mp", None),
        P("section", "dp", "mp", None),
        P("section", None),
        P("section", None),
        P("section"),
        P("section", None, "mp"),
        P("section", None, "mp"),
        P("section", None, "mp"),
        P("section", None, "mp"),
        P("section", "dp", None, "mp"),
        P("section", "dp", None, "mp"),
        P("section", "dp", None, "mp"),
        P("dp", None),
        P("dp", None, None),
        P(),
        P(),
    )
    out_specs = (
        P("section", "dp", "mp", None),
        P("section", "dp", "mp"),
        P("section", "dp", "mp"),
        P("section", "dp", "mp"),
        P("section", "dp", "mp"),
        P("dp", ("section", "mp"), None),
    )
    return jax.shard_map(
        per_device, mesh=mesh, in_specs=in_specs, out_specs=out_specs, check_vma=False
    )
```

time: 551 us -> 394 us (0.72); the launches traced: 540 us -> 394 us
  matrix products: 130 us -> 27.2 us
  Pallas kernels: 0 us -> 86.4 us
  waiting for transfers between devices: 268 us -> 218 us
  other arithmetic: 57.6 us -> 21.4 us
  local copies, waits for them, and re-layouts: 47 us -> 13.2 us
  starting transfers between devices: 21.5 us -> 12.8 us
    dot_general x64 -> x2, matrix products: 107 us -> 3.74 us  [the longest x1 2.63 us: relay(): jnp.einsum('thd,nhd->htn', split(query), split(key), preferred_element_ty...]
    pallas_call x0 -> x1, Pallas kernels: none -> 86.4 us  [relay(): pl.pallas_call(functools.partial(relay_kernel, sections), out_shape=(shap...]
    ppermute x7 -> x0, waiting for transfers between devices: 76.5 us -> none  [shifted(): return lax.ppermute(x, axis, pairs)]
    unnamed x12 -> x0, other arithmetic: 26.9 us -> none
    reduce_scatter x3, waiting for transfers between devices: 38.3 us -> 59 us  [scattered(): lax.psum_scatter(x.astype(bf16), 'dp', scatter_dimension=0, tiled=True)]
    unnamed x226 -> x33, local copies, waits for them, and re-layouts: 19.8 us -> 6.78 us
    dot_general x13 -> x0, other arithmetic: 12.7 us -> none  [relay(): jnp.einsum('thd,thd->ht', ga3.astype(f32), cut(attended[k]).astype(f32))]
    convert_element_type x14 -> x0, local copies, waits for them, and re-layouts: 12.5 us -> none  [relay(): ga_k = (gate * jnp.dot(dy, w_o[k], preferred_element_type=f32)).astype(bf16)]
  transfers between devices with their start and end apart: 20 -> 13, of which waited for: 12 -> 9; matrix products, arithmetic and copies ran while one was open for 16% -> 13% of each run, Pallas kernels for 0% -> 0%
where the time goes in v2:
time: 394 us
  waiting for transfers between devices  218 us (55%)
  Pallas kernels  86.4 us (22%)
  matrix products  27.2 us (7%)
  other arithmetic  21.4 us (5%)
  between operations  14.8 us (4%)
  local copies, waits for them, and re-layouts  13.2 us (3%)
  starting transfers between devices  12.8 us (3%)
    ppermute x9, waiting for transfers between devices, from_ahead(): return lax.ppermute(x, axis, pairs)  159 us
    pallas_call x1, Pallas kernels, relay(): pl.pallas_call(functools.partial(relay_kernel, sections), out_shape=(shap...  86.4 us
    reduce_scatter x3, waiting for transfers between devices, scattered(): lax.psum_scatter(x.astype(bf16), 'dp', scatter_dimension=0, tiled=True)  59 us
    dot_general x5, matrix products, over_rows(): lax.dot_general(left, right, contract_rows, preferred_element_type=f32)  21.5 us
    ppermute x9, starting transfers between devices, from_ahead(): return lax.ppermute(x, axis, pairs)  12.5 us
  transfers between devices with their start and end apart: 13, of which 9 were waited for; matrix products, arithmetic and copies ran while one was open for 13% of the time, Pallas kernels for 0%

profile of v2, /device:TPU:0, one launch (start us, length us, event | category | flops | bytes accessed | tf_op | source)
XLA Modules:
  0.0 394.1 jit_solution(1405840605052028259)
XLA Ops:
  8.4 3.0 collective-permute-start
  11.5 1.9 collective-permute-start.2
  13.5 1.9 collective-permute-start.4
  15.5 3.0 convert_reduce_fusion
  18.9 1.2 fusion.2
  24.3 1.3 collective-permute-done.2
  25.9 2.6 select_reduce_fusion
  28.6 1.9 fusion.9
  30.5 1.8 divide_convert_fusion.probs_ref
  36.1 34.5 %collective-permute-done.3 = bf16[4096,256]{1,0:T(8,128)(2,1)} collective-permute-done((bf16[4096,256]{1,0:T(8,128)(2,1)}, bf16[4096,256]{1,0:T(8,128)(2,1)}, u32[]{:S(2)}, u32[]{:S(2)}) %collective-permute-start.3) | collective-permute-done | bytes 2097184 | tf_op jit(solution)/shard_map/ppermute | solution.py:34
  70.6 4.5 %pad_maximum_fusion.w_o_ref = bf16[4096,512]{1,0:T(8,128)(2,1)} fusion(bf16[4096,256]{1,0:T(8,128)(2,1)} %collective-permute-done.3, bf16[4096,256]{1,0:T(8,128)(2,1)} %bitcast.64), kind=kLoop, calls=%fused_computation.18 | loop fusion | flops 8388608 | bytes 8388608 | tf_op jit(solution)/shard_map/concatenate | solution.py:281
  75.1 39.6 %collective-permute-done.4 = bf16[4096,256]{1,0:T(8,128)(2,1)} collective-permute-done((bf16[4096,256]{1,0:T(8,128)(2,1)}, bf16[4096,256]{1,0:T(8,128)(2,1)}, u32[]{:S(2)}, u32[]{:S(2)}) %collective-permute-start.4) | collective-permute-done | bytes 2097184 | tf_op jit(solution)/shard_map/ppermute | solution.py:34
  114.7 3.8 pad_maximum_fusion.1.w_q_ref
  118.5 86.4 %relay.1 = (bf16[512,4096]{1,0:T(8,128)(2,1)}, bf16[512,4096]{1,0:T(8,128)(2,1)}, bf16[512,512]{1,0:T(8,128)(2,1)S(1)}, f32[512,320]{1,0:T(8,128)S(1)}, f32[512,320]{1,0:T(8,128)S(1)}) custom-call(f32[1]{0:T(128)} %tanh.6.gate_ref, f32[1,4096]{1,0:T(1,128)S(1)} %copy-done.2, f32[512,1]{1,0:T(8,128)S(1)} %copy.40.mean_ref, f32[512,1]{1,0:T(8,128)S(1)} %copy.41.rstd_ref, ...), custom_call_target="tpu_custom_call" | custom-call | flops 4966055936 | bytes 25165824 | tf_op jit(solution)/shard_map/relay/pallas_call | solution.py:239
  205.0 1.7 collective-permute-start.7
  207.2 5.6 %collective-permute-done.7 = f32[256,320]{1,0:T(8,128)S(1)} collective-permute-done((f32[256,320]{1,0:T(8,128)S(1)}, f32[256,320]{1,0:T(8,128)S(1)}, u32[]{:S(2)}, u32[]{:S(2)}) %collective-permute-start.7) | collective-permute-done | bytes 327712 | tf_op jit(solution)/shard_map/ppermute | solution.py:34
  213.3 3.7 collective-permute-done.6
  217.1 1.5 fusion.12
  219.1 4.8 %fusion.8 = bf16[4096,256]{1,0:T(8,128)(2,1)} fusion(bf16[512,4096]{1,0:T(8,128)(2,1)} %get-tuple-element.15, f32[]{:T(128)} %bitcast.30, bf16[512,512]{0,1:T(8,128)(2,1)S(1)} %bitcast.68), kind=kOutput, calls=%fused_computation.15 | convolution fusion | flops 1075838976 | bytes 6553604 | tf_op jit(solution)/shard_map/dot_general | solution.py:347
  223.9 1.6 collective-permute-start.8
  225.9 1.9 convolution_convert_fusion.1
  227.9 40.3 %collective-permute-done.8 = bf16[4096,256]{1,0:T(8,128)(2,1)} collective-permute-done((bf16[4096,256]{1,0:T(8,128)(2,1)}, bf16[4096,256]{1,0:T(8,128)(2,1)}, u32[]{:S(2)}, u32[]{:S(2)}) %collective-permute-start.8) | collective-permute-done | bytes 2097184 | tf_op jit(solution)/shard_map/ppermute | solution.py:34
  268.2 5.7 %fusion.7 = bf16[4096,256]{1,0:T(8,128)(2,1)} fusion(bf16[512,4096]{1,0:T(8,128)(2,1)} %get-tuple-element.15, bf16[4096,256]{1,0:T(8,128)(2,1)} %collective-permute-done.8, f32[]{:T(128)} %bitcast.30, bf16[512,512]{0,1:T(8,128)(2,1)S(1)} %bitcast.69), kind=kOutput, calls=%fused_computation.14 | convolution fusion | flops 1077936128 | bytes 8650756 | tf_op jit(solution)/shard_map/dot_general | solution.py:347
  274.0 4.9 %convolution_convert_fusion = bf16[4096,256]{1,0:T(8,128)(2,1)S(1)} fusion(bf16[512,512]{1,0:T(8,128)(2,1)S(1)} %get-tuple-element.12, f32[4096]{0:T(1024)S(1)} %bitcast.88, f32[4096]{0:T(1024)S(1)} %bitcast.57, f32[512]{0:T(512)S(1)} %add_rsqrt_fusion.1, f32[512]{0:T(512)S(1)} %broadcast_multiply_fusion.1, bf16[1,1,512,4096]{3,2,1,0:T(8,128)(2,1)} %param.17), kind=kOutput, calls=%fused_computation.16 | convolution fusion | flops 1087373312 | bytes 6590464 | tf_op jit(solution)/shard_map/dot_general | solution.py:347
  278.9 1.7 collective-permute-start.5
  280.6 34.4 %collective-permute-done.5 = bf16[4096,256]{1,0:T(8,128)(2,1)S(1)} collective-permute-done((bf16[4096,256]{1,0:T(8,128)(2,1)S(1)}, bf16[4096,256]{1,0:T(8,128)(2,1)S(1)}, u32[]{:S(2)}, u32[]{:S(2)}) %collective-permute-start.5) | collective-permute-done | bytes 2097184 | tf_op jit(solution)/shard_map/ppermute | solution.py:34
  314.9 4.1 %add_convert_fusion = bf16[4096,256]{1,0:T(8,128)(2,1)} fusion(bf16[4096,256]{1,0:T(8,128)(2,1)S(1)} %collective-permute-done.5, bf16[512,512]{1,0:T(8,128)(2,1)S(1)} %get-tuple-element.12, f32[4096]{0:T(1024)S(1)} %bitcast.89, f32[4096]{0:T(1024)S(1)} %bitcast.58, f32[512]{0:T(512)S(1)} %add_rsqrt_fusion.1, f32[512]{0:T(512)S(1)} %broadcast_multiply_fusion.1, ...), kind=kOutput, calls=%fused_computation.20 | convolution fusion | flops 1089470464 | bytes 8687616 | tf_op jit(solution)/shard_map/dot_general | solution.py:347
  320.5 1.7 subtract_multiply_fusion
  322.2 1.7 slice_bitcast_fusion
  323.8 13.1 %reduce-scatter.9.cloned.1.call-done = bf16[1024,256]{1,0:T(8,128)(2,1)} async-done(((bf16[4096,256]{1,0:T(8,128)(2,1)}), bf16[1024,256]{1,0:T(8,128)(2,1)}) %reduce-scatter.9.cloned.1.call-update) | async-done | bytes 524304 | tf_op jit(solution)/shard_map/reduce_scatter | solution.py:350
  336.9 45.9 %reduce-scatter.5.cloned.1.call-done = bf16[1024,256]{1,0:T(8,128)(2,1)} async-done(((bf16[4096,256]{1,0:T(8,128)(2,1)}), bf16[1024,256]{1,0:T(8,128)(2,1)}) %reduce-scatter.5.cloned.1.call-update) | async-done | bytes 524304 | tf_op jit(solution)/shard_map/reduce_scatter | solution.py:350
  382.8 4.8 %copy.47 = bf16[1,1,512,4096]{3,2,1,0:T(8,128)(2,1)} copy(bf16[1,1,512,4096]{3,2,1,0:T(8,128)(2,1)} %bitcast.60) | data formatting | bytes 8388608
  (82 shorter events, 12.7 us)
Async XLA Ops:
  7.2 205.7 %copy-start = (bf16[1,1024,256]{2,1,0:T(8,128)(2,1)S(1)}, bf16[1,1024,256]{2,1,0:T(8,128)(2,1)}, u32[]{:S(2)}) copy-start(bf16[1,1024,256]{2,1,0:T(8,128)(2,1)} %param.23) | copy-start | bytes 1572868
  7.2 312.2 %reduce-scatter.11.cloned.1.call-start = ((), (), s32[]{:S(2)}) async-start(), calls=%async_computation.7 | async-start | bytes 1474560 | tf_op jit(solution)/shard_map/reduce_scatter | solution.py:365
  8.4 17.4 %collective-permute-start = (bf16[512,256]{1,0:T(8,128)(2,1)S(1)}, bf16[512,256]{1,0:T(8,128)(2,1)S(1)}, u32[]{:S(2)}, u32[]{:S(2)}) collective-permute-start(bf16[512,256]{1,0:T(8,128)(2,1)S(1)} %get-tuple-element.19), channel_id=1, source_target_pairs={{4,0},{0,4},{5,1},{1,5},{6,2},{2,6},{7,3},{3,7},{12,8},{8,12},{13,... | collective-permute-start | bytes 786440 | tf_op jit(solution)/shard_map/ppermute | solution.py:34
  11.4 12.1 %collective-permute-start.1 = (bf16[320,256]{1,0:T(8,128)(2,1)}, bf16[320,256]{1,0:T(8,128)(2,1)S(1)}, u32[]{:S(2)}, u32[]{:S(2)}) collective-permute-start(bf16[320,256]{1,0:T(8,128)(2,1)} %bitcast.75), channel_id=1, source_target_pairs={{4,0},{0,4},{5,1},{1,5},{6,2},{2,6},{7,3},{3,7},{12,8},{8,12},{13,... | collective-permute-start | bytes 491528 | tf_op jit(solution)/shard_map/ppermute | solution.py:34
  11.5 14.1 %collective-permute-start.2 = (bf16[320,256]{1,0:T(8,128)(2,1)}, bf16[320,256]{1,0:T(8,128)(2,1)S(1)}, u32[]{:S(2)}, u32[]{:S(2)}) collective-permute-start(bf16[320,256]{1,0:T(8,128)(2,1)} %bitcast.77), channel_id=1, source_target_pairs={{4,0},{0,4},{5,1},{1,5},{6,2},{2,6},{7,3},{3,7},{12,8},{8,12},{13,... | collective-permute-start | bytes 491528 | tf_op jit(solution)/shard_map/ppermute | solution.py:34
  13.4 57.2 %collective-permute-start.3 = (bf16[4096,256]{1,0:T(8,128)(2,1)}, bf16[4096,256]{1,0:T(8,128)(2,1)}, u32[]{:S(2)}, u32[]{:S(2)}) collective-permute-start(bf16[4096,256]{1,0:T(8,128)(2,1)} %bitcast.63), channel_id=1, source_target_pairs={{4,0},{0,4},{5,1},{1,5},{6,2},{2,6},{7,3},{3,7},{12,8},{8,12},{13,... | collective-permute-start | bytes 6291464 | tf_op jit(solution)/shard_map/ppermute | solution.py:34
  13.5 101.2 %collective-permute-start.4 = (bf16[4096,256]{1,0:T(8,128)(2,1)}, bf16[4096,256]{1,0:T(8,128)(2,1)}, u32[]{:S(2)}, u32[]{:S(2)}) collective-permute-start(bf16[4096,256]{1,0:T(8,128)(2,1)} %bitcast.65), channel_id=1, source_target_pairs={{4,0},{0,4},{5,1},{1,5},{6,2},{2,6},{7,3},{3,7},{12,8},{8,12},{13,... | collective-permute-start | bytes 6291464 | tf_op jit(solution)/shard_map/ppermute | solution.py:34
  15.4 3.4 copy-start.3
  15.4 4.7 %copy-start.12 = (s32[1,1024]{1,0:T(1,128)S(1)}, s32[1,1024]{1,0:T(1,128)}, u32[]{:S(2)}) copy-start(s32[1,1024]{1,0:T(1,128)} %param.28) | copy-start | bytes 12292
  15.4 5.0 %copy-start.8 = (bf16[1,1,320,256]{3,2,1,0:T(8,128)(2,1)S(1)}, bf16[1,1,320,256]{3,2,1,0:T(8,128)(2,1)}, u32[]{:S(2)}) copy-start(bf16[1,1,320,256]{3,2,1,0:T(8,128)(2,1)} %param.26) | copy-start | bytes 491524
  15.5 5.8 %copy-start.9 = (bf16[1,1,320,256]{3,2,1,0:T(8,128)(2,1)S(1)}, bf16[1,1,320,256]{3,2,1,0:T(8,128)(2,1)}, u32[]{:S(2)}) copy-start(bf16[1,1,320,256]{3,2,1,0:T(8,128)(2,1)} %param.27) | copy-start | bytes 491524
  32.3 1.6 copy-start.5
  36.1 78.6 %copy-start.7 = (bf16[1,4096,256]{2,1,0:T(8,128)(2,1)S(1)}, bf16[1,4096,256]{2,1,0:T(8,128)(2,1)}, u32[]{:S(2)}) copy-start(bf16[1,4096,256]{2,1,0:T(8,128)(2,1)} %param.21) | copy-start | bytes 6291460
  75.1 43.4 %copy-start.2 = (f32[1,4096]{1,0:T(1,128)S(1)}, f32[1,4096]{1,0:T(1,128)}, u32[]{:S(2)}) copy-start(f32[1,4096]{1,0:T(1,128)} %gain_ref.1) | copy-start | bytes 49156
  204.9 12.1 %copy-start.10 = (bf16[1,1024,256]{2,1,0:T(8,128)(2,1)S(1)}, bf16[1,1024,256]{2,1,0:T(8,128)(2,1)}, u32[]{:S(2)}) copy-start(bf16[1,1024,256]{2,1,0:T(8,128)(2,1)} %param.22) | copy-start | bytes 1572868
  205.0 7.8 %collective-permute-start.7 = (f32[256,320]{1,0:T(8,128)S(1)}, f32[256,320]{1,0:T(8,128)S(1)}, u32[]{:S(2)}, u32[]{:S(2)}) collective-permute-start(f32[256,320]{1,0:T(8,128)S(1)} %split.29), channel_id=1, source_target_pairs={{4,0},{0,4},{5,1},{1,5},{6,2},{2,6},{7,3},{3,7},{12,8},{8,12},{13,... | collective-permute-start | bytes 983048 | tf_op jit(solution)/shard_map/ppermute | solution.py:34
  206.6 12.2 %copy-start.6 = (bf16[1,320,1024]{2,1,0:T(8,128)(2,1)S(1)}, bf16[1,320,1024]{2,1,0:T(8,128)(2,1)}, u32[]{:S(2)}) copy-start(bf16[1,320,1024]{2,1,0:T(8,128)(2,1)} %param.29) | copy-start | bytes 1966084
  206.7 10.3 %collective-permute-start.6 = (f32[256,320]{1,0:T(8,128)S(1)}, f32[256,320]{1,0:T(8,128)S(1)}, u32[]{:S(2)}, u32[]{:S(2)}) collective-permute-start(f32[256,320]{1,0:T(8,128)S(1)} %split.27), channel_id=1, source_target_pairs={{4,0},{0,4},{5,1},{1,5},{6,2},{2,6},{7,3},{3,7},{12,8},{8,12},{13,... | collective-permute-start | bytes 983048 | tf_op jit(solution)/shard_map/ppermute | solution.py:34
  218.6 103.5 %reduce-scatter.7.cloned.1.call-start = ((), (), s32[]{:S(2)}) async-start(), calls=%async_computation.5 | async-start | bytes 1310720 | tf_op jit(solution)/shard_map/reduce_scatter | solution.py:350
  219.1 6.8 %copy-start.11 = (f32[1024]{0:T(1024)S(1)}, f32[1024]{0:T(1024)}, u32[]{:S(2)}) copy-start(f32[1024]{0:T(1024)} %param.30) | copy-start | bytes 12292
  219.1 6.8 %copy-start.14 = (f32[1024]{0:T(1024)S(1)}, f32[1024]{0:T(1024)}, u32[]{:S(2)}) copy-start(f32[1024]{0:T(1024)} %param.31) | copy-start | bytes 12292
  223.9 44.2 %collective-permute-start.8 = (bf16[4096,256]{1,0:T(8,128)(2,1)}, bf16[4096,256]{1,0:T(8,128)(2,1)}, u32[]{:S(2)}, u32[]{:S(2)}) collective-permute-start(bf16[4096,256]{1,0:T(8,128)(2,1)} %fusion.8), channel_id=1, source_target_pairs={{4,0},{0,4},{5,1},{1,5},{6,2},{2,6},{7,3},{3,7},{12,8},{8,12},{13,... | collective-permute-start | bytes 6291464 | tf_op jit(solution)/shard_map/ppermute | solution.py:34
  227.8 46.1 %copy-start.13 = (f32[1,4096]{1,0:T(1,128)S(1)}, f32[1,4096]{1,0:T(1,128)}, u32[]{:S(2)}) copy-start(f32[1,4096]{1,0:T(1,128)} %param.19) | copy-start | bytes 49156
  227.8 109.1 %reduce-scatter.9.cloned.1.call-start = ((), (), s32[]{:S(2)}) async-start(), calls=%async_computation.6 | async-start | bytes 2621440 | tf_op jit(solution)/shard_map/reduce_scatter | solution.py:350
  273.9 108.9 %reduce-scatter.5.cloned.1.call-start = ((), (), s32[]{:S(2)}) async-start(), calls=%async_computation.4 | async-start | bytes 2621440 | tf_op jit(solution)/shard_map/reduce_scatter | solution.py:350
  274.0 40.9 %copy-start.4 = (bf16[1,1,512,4096]{3,2,1,0:T(8,128)(2,1)S(1)}, bf16[1,1,512,4096]{3,2,1,0:T(8,128)(2,1)}, u32[]{:S(2)}) copy-start(bf16[1,1,512,4096]{3,2,1,0:T(8,128)(2,1)} %param.17) | copy-start | bytes 12582916
  278.9 36.0 %collective-permute-start.5 = (bf16[4096,256]{1,0:T(8,128)(2,1)S(1)}, bf16[4096,256]{1,0:T(8,128)(2,1)S(1)}, u32[]{:S(2)}, u32[]{:S(2)}) collective-permute-start(bf16[4096,256]{1,0:T(8,128)(2,1)S(1)} %convolution_convert_fusion), channel_id=1, source_target_pairs={{4,0},{0,4},{5,1},{1,5},{6,2},{2,6},{7,3},{3,7},{12,8},{8,12},{13,... | collective-permute-start | bytes 6291464 | tf_op jit(solution)/shard_map/ppermute | solution.py:34
  382.8 4.8 %copy-start.1 = (bf16[1,1024,256]{2,1,0:T(8,128)(2,1)S(1)}, bf16[1,1024,256]{2,1,0:T(8,128)(2,1)}, u32[]{:S(2)}) copy-start(bf16[1,1024,256]{2,1,0:T(8,128)(2,1)} %param.23) | copy-start | bytes 1572868
Sparse Core Ops, SparseCore 0:
  218.8 42.1 reduce-scatter.10
  263.2 28.0 reduce-scatter.6
  294.3 42.5 reduce-scatter.8
  339.6 43.1 reduce-scatter.4

commit v3 on v2

--- a/solution.py
+++ b/solution.py
@@ -40,6 +40,7 @@
 
 def relay_kernel(
     sections,
+    ways,
     gate_ref,
     gain_ref,
     mean_ref,
@@ -50,24 +51,12 @@
     key_ref,
     value_ref,
     x_ref,
-    w_o_ref,
-    w_q_ref,
-    up_ref,
-    dy_out,
-    dx_out,
-    gq_ref,
-    gk_ref,
-    gv_ref,
-    dy_buf,
-    dx_buf,
-    back_buf,
-    gs_buf,
-    up_sem,
-    send_sem,
-    recv_sem,
-    dy_sem,
-    dx_sem,
+    *rest,
 ):
+    w_o_refs, w_q_refs = rest[:ways], rest[ways : 2 * ways]
+    up_ref, dy_out, dx_out, gq_ref, gk_ref, gv_ref = rest[2 * ways : 2 * ways + 6]
+    dy_buf, dx_buf, back_buf, gs_buf = rest[2 * ways + 6 : 2 * ways + 10]
+    up_sem, send_sem, recv_sem, dy_sem, dx_sem = rest[2 * ways + 10 :]
     f32 = jnp.float32
     bf16 = jnp.bfloat16
     section_at = lax.axis_index("section")
@@ -135,7 +124,9 @@
             hop(i).wait_recv()
 
         dy_store(i).start()
-        ga32 = gate * jnp.dot(dy_buf[r, :], w_o_ref[...], preferred_element_type=f32)
+        ga32 = gate * jnp.concatenate(
+            [jnp.dot(dy_buf[r, :], w[...], preferred_element_type=f32) for w in w_o_refs], 1
+        )
         ga = ga32.astype(bf16)
         ga_r = ga.astype(f32)
         ga_t = ga32.T.astype(bf16)
@@ -155,9 +146,14 @@
 
         def back(c, carry):
             cols = pl.ds(pl.multiple_of(c * chunk, chunk), chunk)
-            back_buf[:, cols] = lax.dot_general(
-                gq_ref[r, :], w_q_ref[cols, :], nt, preferred_element_type=f32
-            )
+            total = None
+            for k in range(ways):
+                f = slice(k * inner // ways, (k + 1) * inner // ways)
+                part = lax.dot_general(
+                    gq_ref[r, f], w_q_refs[k][cols, :], nt, preferred_element_type=f32
+                )
+                total = part if total is None else total + part
+            back_buf[:, cols] = total
             return carry
 
         lax.fori_loop(0, width // chunk, back, 0)
@@ -237,7 +233,7 @@
     hbm = pl.BlockSpec(memory_space=pl.ANY)
     shape = jax.ShapeDtypeStruct
     dy_all, dx_all, gq, gk_t, gv_t = pl.pallas_call(
-        functools.partial(relay_kernel, sections),
+        functools.partial(relay_kernel, sections, ways),
         out_shape=(
             shape((rows, width), bf16),
             shape((rows, width), bf16),
@@ -245,7 +241,7 @@
             shape((inner, n_vis), f32),
             shape((inner, n_vis), f32),
         ),
-        in_specs=[pl.BlockSpec(memory_space=pltpu.SMEM)] + [vmem] * 11 + [hbm],
+        in_specs=[pl.BlockSpec(memory_space=pltpu.SMEM)] + [vmem] * (9 + 2 * ways) + [hbm],
         out_specs=(hbm, hbm, vmem, vmem, vmem),
         scratch_shapes=[
             pltpu.VMEM((rows, width), bf16),
@@ -278,8 +274,8 @@
         key,
         value,
         input_rows,
-        jnp.concatenate(w_o, 1),
-        jnp.concatenate(w_q, 1),
+        *w_o,
+        *w_q,
         grad_rows,
     )
 
@@ -349,10 +345,24 @@
     def scattered(x):
         return lax.psum_scatter(x.astype(bf16), "dp", scatter_dimension=0, tiled=True)
 
+    def homed_scatter(parts):
+        length = lax.axis_size("dp")
+        dp_at = lax.axis_index("dp")
+        share = width // length
+        total = None
+        for k in [*range(1, length), 0]:
+            start = ((dp_at + k) % length) * share
+            cuts = [lax.dynamic_slice_in_dim(part, start, share, 0) for part in parts]
+            block = homed(cuts, bf16)
+            if k:
+                block = from_ahead(block.astype(bf16), "dp", -k).astype(f32)
+            total = block if total is None else total + block
+        return total.astype(bf16)
+
     key_b = homed(gk, f32).T.astype(bf16)
     value_b = homed(gv, f32).T.astype(bf16)
-    out_grad = scattered(homed([gate * over_rows(dy_all, a) for a in att], bf16))
-    query_grad = scattered(homed([over_rows(norm_rows, g) for g in gq], bf16))
+    out_grad = homed_scatter([(gate * over_rows(dy_all, a)).astype(bf16) for a in att])
+    query_grad = homed_scatter([over_rows(norm_rows, g).astype(bf16) for g in gq])
     visual32, lat_normed, lat_rstd = norm_forward(latents.astype(f32), res_gain, res_bias)
     visual = visual32.astype(bf16)[0]
     both = scattered(

time: 394 us -> 388 us (0.985)
  waiting for transfers between devices: 218 us -> 175 us
  starting transfers between devices: 12.8 us -> 54.1 us
  matrix products: 27.2 us -> 18.9 us
    reduce_scatter x3 -> x1, waiting for transfers between devices: 59 us -> 0.01 us  [scattered(): lax.psum_scatter(x.astype(bf16), 'dp', scatter_dimension=0, tiled=True)]
    ppermute x9 -> x21, starting transfers between devices: 12.5 us -> 53.9 us  [from_ahead(): return lax.ppermute(x, axis, pairs)]
    ppermute x9 -> x21, waiting for transfers between devices: 159 us -> 175 us  [from_ahead(): return lax.ppermute(x, axis, pairs)]
    concatenate x2 -> x0, other arithmetic: 8.37 us -> none  [the longest x1 4.54 us: relay(): jnp.concatenate(w_o, 1)]
    dot_general x5, matrix products: 21.5 us -> 13.2 us  [over_rows(): lax.dot_general(left, right, contract_rows, preferred_element_type=f32)]
  transfers between devices with their start and end apart: 13 -> 23, of which waited for: 9 -> 13; matrix products, arithmetic and copies ran while one was open for 13% -> 12% of each run, Pallas kernels for 0% -> 0%
where the time goes in v3:
time: 388 us
  waiting for transfers between devices  175 us (45%)
  Pallas kernels  86.4 us (22%)
  starting transfers between devices  54.1 us (14%)
  other arithmetic  20.8 us (5%)
  matrix products  18.9 us (5%)
  local copies, waits for them, and re-layouts  16.9 us (4%)
  between operations  15.3 us (4%)
    ppermute x21, waiting for transfers between devices, from_ahead(): return lax.ppermute(x, axis, pairs)  175 us
    pallas_call x1, Pallas kernels, relay(): pl.pallas_call(functools.partial(relay_kernel, sections, ways), out_shape...  86.4 us
    ppermute x21, starting transfers between devices, from_ahead(): return lax.ppermute(x, axis, pairs)  53.9 us
    dot_general x5, matrix products, over_rows(): lax.dot_general(left, right, contract_rows, preferred_element_type=f32)  13.2 us
  transfers between devices with their start and end apart: 23, of which 13 were waited for; matrix products, arithmetic and copies ran while one was open for 12% of the time, Pallas kernels for 0%

profile of v3, /device:TPU:0, one launch (start us, length us, event | category | flops | bytes accessed | tf_op | source)
XLA Modules:
  0.0 387.5 jit_solution(6910712828407815635)
XLA Ops:
  7.3 1.8 constant_dynamic-slice_fusion.8
  9.1 2.9 collective-permute-start
  12.1 2.0 collective-permute-start.2
  14.1 2.0 collective-permute-start.4
  16.1 3.0 convert_reduce_fusion
  26.8 2.7 select_reduce_fusion
  29.5 1.9 fusion.8
  31.4 1.8 divide_convert_fusion.probs_ref
  35.4 36.0 %collective-permute-done.3.rest_1_ = bf16[4096,256]{1,0:T(8,128)(2,1)} collective-permute-done((bf16[4096,256]{1,0:T(8,128)(2,1)}, bf16[4096,256]{1,0:T(8,128)(2,1)}, u32[]{:S(2)}, u32[]{:S(2)}) %collective-permute-start.3) | collective-permute-done | bytes 2097184 | tf_op jit(solution)/shard_map/ppermute | solution.py:34
  71.4 44.1 %collective-permute-done.4.rest_3_ = bf16[4096,256]{1,0:T(8,128)(2,1)} collective-permute-done((bf16[4096,256]{1,0:T(8,128)(2,1)}, bf16[4096,256]{1,0:T(8,128)(2,1)}, u32[]{:S(2)}, u32[]{:S(2)}) %collective-permute-start.4) | collective-permute-done | bytes 2097184 | tf_op jit(solution)/shard_map/ppermute | solution.py:34
  115.6 86.4 %relay.1 = (bf16[512,4096]{1,0:T(8,128)(2,1)}, bf16[512,4096]{1,0:T(8,128)(2,1)}, bf16[512,512]{1,0:T(8,128)(2,1)S(1)}, f32[512,320]{1,0:T(8,128)S(1)}, f32[512,320]{1,0:T(8,128)S(1)}) custom-call(f32[1]{0:T(128)} %tanh.6.gate_ref, f32[1,4096]{1,0:T(1,128)S(1)} %copy-done.3, f32[512,1]{1,0:T(8,128)S(1)} %copy.40.mean_ref, f32[512,1]{1,0:T(8,128)S(1)} %copy.41.rstd_ref, ...), custom_call_target="tpu_custom_call" | custom-call | flops 4966055936 | bytes 25165824 | tf_op jit(solution)/shard_map/relay/pallas_call | solution.py:235
  205.5 5.3 %collective-permute-done.13 = f32[256,320]{1,0:T(8,128)} collective-permute-done((f32[256,320]{1,0:T(8,128)S(1)}, f32[256,320]{1,0:T(8,128)}, u32[]{:S(2)}, u32[]{:S(2)}) %collective-permute-start.13) | collective-permute-done | bytes 327712 | tf_op jit(solution)/shard_map/ppermute | solution.py:34
  212.5 2.5 collective-permute-done.12
  216.8 3.5 fusion.7
  225.8 2.5 convolution_convert_fusion
  231.4 2.6 fusion.6
  234.1 2.0 convolution_convert_fusion.2
  238.5 13.1 %collective-permute-done.16 = bf16[1024,256]{1,0:T(8,128)(2,1)} collective-permute-done((bf16[1024,256]{1,0:T(8,128)(2,1)}, bf16[1024,256]{1,0:T(8,128)(2,1)}, u32[]{:S(2)}, u32[]{:S(2)}) %collective-permute-start.16) | collective-permute-done | bytes 524320 | tf_op jit(solution)/shard_map/ppermute | solution.py:34
  253.3 11.4 %collective-permute-done.18 = bf16[1024,256]{1,0:T(8,128)(2,1)} collective-permute-done((bf16[1024,256]{1,0:T(8,128)(2,1)}, bf16[1024,256]{1,0:T(8,128)(2,1)}, u32[]{:S(2)}, u32[]{:S(2)}) %collective-permute-start.18) | collective-permute-done | bytes 524320 | tf_op jit(solution)/shard_map/ppermute | solution.py:34
  264.6 2.3 add_convert_fusion.4
  268.6 18.5 %collective-permute-done.5 = bf16[1024,256]{1,0:T(8,128)(2,1)} collective-permute-done((bf16[1024,256]{1,0:T(8,128)(2,1)}, bf16[1024,256]{1,0:T(8,128)(2,1)}, u32[]{:S(2)}, u32[]{:S(2)}) %collective-permute-start.5) | collective-permute-done | bytes 524320 | tf_op jit(solution)/shard_map/ppermute | solution.py:34
  287.1 2.7 collective-permute-start.17
  289.8 2.5 convolution_convert_fusion.1
  292.3 5.9 %collective-permute-done.7 = bf16[1024,256]{1,0:T(8,128)(2,1)S(1)} collective-permute-done((bf16[1024,256]{1,0:T(8,128)(2,1)}, bf16[1024,256]{1,0:T(8,128)(2,1)S(1)}, u32[]{:S(2)}, u32[]{:S(2)}) %collective-permute-start.7) | collective-permute-done | bytes 524320 | tf_op jit(solution)/shard_map/ppermute | solution.py:34
  299.8 5.4 %collective-permute-done.9 = bf16[1024,256]{1,0:T(8,128)(2,1)S(1)} collective-permute-done((bf16[1024,256]{1,0:T(8,128)(2,1)S(1)}, bf16[1024,256]{1,0:T(8,128)(2,1)S(1)}, u32[]{:S(2)}, u32[]{:S(2)}) %collective-permute-start.9) | collective-permute-done | bytes 524320 | tf_op jit(solution)/shard_map/ppermute | solution.py:34
  305.2 3.7 collective-permute-start.19
  310.8 13.9 %collective-permute-start.6 = (bf16[1024,256]{1,0:T(8,128)(2,1)S(1)}, bf16[1024,256]{1,0:T(8,128)(2,1)S(1)}, u32[]{:S(2)}, u32[]{:S(2)}) collective-permute-start(bf16[1024,256]{1,0:T(8,128)(2,1)S(1)} %get-tuple-element.25), channel_id=1, source_target_pairs={{3,0},{0,1},{1,2},{2,3},{7,4},{4,5},{5,6},{6,7},{11,8},{8,9},{9,10... | collective-permute-start | bytes 1572872 | tf_op jit(solution)/shard_map/ppermute | solution.py:34
  324.8 11.7 %collective-permute-start.8 = (bf16[1024,256]{1,0:T(8,128)(2,1)S(1)}, bf16[1024,256]{1,0:T(8,128)(2,1)S(1)}, u32[]{:S(2)}, u32[]{:S(2)}) collective-permute-start(bf16[1024,256]{1,0:T(8,128)(2,1)S(1)} %get-tuple-element.27), channel_id=1, source_target_pairs={{2,0},{3,1},{0,2},{1,3},{6,4},{7,5},{4,6},{5,7},{10,8},{11,9},{8,1... | collective-permute-start | bytes 1572872 | tf_op jit(solution)/shard_map/ppermute | solution.py:34
  336.7 2.3 fusion.18
  339.9 30.4 %collective-permute-done.8 = bf16[1024,256]{1,0:T(8,128)(2,1)S(1)} collective-permute-done((bf16[1024,256]{1,0:T(8,128)(2,1)S(1)}, bf16[1024,256]{1,0:T(8,128)(2,1)S(1)}, u32[]{:S(2)}, u32[]{:S(2)}) %collective-permute-start.8) | collective-permute-done | bytes 524320 | tf_op jit(solution)/shard_map/ppermute | solution.py:34
  372.6 1.7 subtract_multiply_fusion
  375.9 4.8 %copy.47 = bf16[1,1,512,4096]{3,2,1,0:T(8,128)(2,1)} copy(bf16[1,1,512,4096]{3,2,1,0:T(8,128)(2,1)} %bitcast.62) | data formatting | bytes 8388608
  (134 shorter events, 38.7 us)
Async XLA Ops:
  7.2 204.9 %copy-start = (bf16[1,1024,256]{2,1,0:T(8,128)(2,1)S(1)}, bf16[1,1024,256]{2,1,0:T(8,128)(2,1)}, u32[]{:S(2)}) copy-start(bf16[1,1024,256]{2,1,0:T(8,128)(2,1)} %param.23) | copy-start | bytes 1572868
  7.2 364.3 %reduce-scatter.5.cloned.1.call-start = ((), (), s32[]{:S(2)}) async-start(), calls=%async_computation.3 | async-start | bytes 1474560 | tf_op jit(solution)/shard_map/reduce_scatter | solution.py:375
  9.1 17.5 %collective-permute-start = (bf16[512,256]{1,0:T(8,128)(2,1)}, bf16[512,256]{1,0:T(8,128)(2,1)S(1)}, u32[]{:S(2)}, u32[]{:S(2)}) collective-permute-start(bf16[512,256]{1,0:T(8,128)(2,1)} %get-tuple-element.33), channel_id=1, source_target_pairs={{4,0},{0,4},{5,1},{1,5},{6,2},{2,6},{7,3},{3,7},{12,8},{8,12},{13,... | collective-permute-start | bytes 786440 | tf_op jit(solution)/shard_map/ppermute | solution.py:34
  12.0 12.9 %collective-permute-start.1 = (bf16[320,256]{1,0:T(8,128)(2,1)}, bf16[320,256]{1,0:T(8,128)(2,1)S(1)}, u32[]{:S(2)}, u32[]{:S(2)}) collective-permute-start(bf16[320,256]{1,0:T(8,128)(2,1)} %bitcast.77), channel_id=1, source_target_pairs={{4,0},{0,4},{5,1},{1,5},{6,2},{2,6},{7,3},{3,7},{12,8},{8,12},{13,... | collective-permute-start | bytes 491528 | tf_op jit(solution)/shard_map/ppermute | solution.py:34
  12.1 14.3 %collective-permute-start.2 = (bf16[320,256]{1,0:T(8,128)(2,1)}, bf16[320,256]{1,0:T(8,128)(2,1)S(1)}, u32[]{:S(2)}, u32[]{:S(2)}) collective-permute-start(bf16[320,256]{1,0:T(8,128)(2,1)} %bitcast.79), channel_id=1, source_target_pairs={{4,0},{0,4},{5,1},{1,5},{6,2},{2,6},{7,3},{3,7},{12,8},{8,12},{13,... | collective-permute-start | bytes 491528 | tf_op jit(solution)/shard_map/ppermute | solution.py:34
  14.0 57.4 %collective-permute-start.3 = (bf16[4096,256]{1,0:T(8,128)(2,1)}, bf16[4096,256]{1,0:T(8,128)(2,1)}, u32[]{:S(2)}, u32[]{:S(2)}) collective-permute-start(bf16[4096,256]{1,0:T(8,128)(2,1)} %bitcast.68), channel_id=1, source_target_pairs={{4,0},{0,4},{5,1},{1,5},{6,2},{2,6},{7,3},{3,7},{12,8},{8,12},{13,... | collective-permute-start | bytes 6291464 | tf_op jit(solution)/shard_map/ppermute | solution.py:34
  14.1 101.4 %collective-permute-start.4 = (bf16[4096,256]{1,0:T(8,128)(2,1)}, bf16[4096,256]{1,0:T(8,128)(2,1)}, u32[]{:S(2)}, u32[]{:S(2)}) collective-permute-start(bf16[4096,256]{1,0:T(8,128)(2,1)} %bitcast.70), channel_id=1, source_target_pairs={{4,0},{0,4},{5,1},{1,5},{6,2},{2,6},{7,3},{3,7},{12,8},{8,12},{13,... | collective-permute-start | bytes 6291464 | tf_op jit(solution)/shard_map/ppermute | solution.py:34
  33.3 82.2 %copy-start.3 = (f32[1,4096]{1,0:T(1,128)S(1)}, f32[1,4096]{1,0:T(1,128)}, u32[]{:S(2)}) copy-start(f32[1,4096]{1,0:T(1,128)} %gain_ref.1) | copy-start | bytes 49156
  35.0 80.6 %copy-start.11 = (bf16[8,64,512]{2,1,0:T(8,128)(2,1)}, bf16[8,64,512]{2,1,0:T(8,128)(2,1)S(1)}, u32[]{:S(2)}) copy-start(bf16[8,64,512]{2,1,0:T(8,128)(2,1)S(1)} %convolution_convert_fusion.3) | copy-start | bytes 1572868
  115.5 89.0 %copy-start.9 = (bf16[1,320,1024]{2,1,0:T(8,128)(2,1)S(1)}, bf16[1,320,1024]{2,1,0:T(8,128)(2,1)}, u32[]{:S(2)}) copy-start(bf16[1,320,1024]{2,1,0:T(8,128)(2,1)} %param.29) | copy-start | bytes 1966084
  115.5 89.0 %copy-start.21 = (f32[320]{0:T(512)S(1)}, f32[320]{0:T(512)}, u32[]{:S(2)}) copy-start(f32[320]{0:T(512)} %broadcast_multiply_fusion) | copy-start | bytes 3844
  202.0 13.0 %copy-start.15 = (bf16[1,1024,256]{2,1,0:T(8,128)(2,1)S(1)}, bf16[1,1024,256]{2,1,0:T(8,128)(2,1)}, u32[]{:S(2)}) copy-start(bf16[1,1024,256]{2,1,0:T(8,128)(2,1)} %param.22) | copy-start | bytes 1572868
  202.9 7.9 %collective-permute-start.13 = (f32[256,320]{1,0:T(8,128)S(1)}, f32[256,320]{1,0:T(8,128)}, u32[]{:S(2)}, u32[]{:S(2)}) collective-permute-start(f32[256,320]{1,0:T(8,128)S(1)} %split.29), channel_id=1, source_target_pairs={{4,0},{0,4},{5,1},{1,5},{6,2},{2,6},{7,3},{3,7},{12,8},{8,12},{13,... | collective-permute-start | bytes 983048 | tf_op jit(solution)/shard_map/ppermute | solution.py:34
  205.1 9.9 %collective-permute-start.12 = (f32[256,320]{1,0:T(8,128)S(1)}, f32[256,320]{1,0:T(8,128)S(1)}, u32[]{:S(2)}, u32[]{:S(2)}) collective-permute-start(f32[256,320]{1,0:T(8,128)S(1)} %split.27), channel_id=1, source_target_pairs={{4,0},{0,4},{5,1},{1,5},{6,2},{2,6},{7,3},{3,7},{12,8},{8,12},{13,... | collective-permute-start | bytes 983048 | tf_op jit(solution)/shard_map/ppermute | solution.py:34
  216.6 157.7 %reduce-scatter.3.cloned.1.call-start = ((), (), s32[]{:S(2)}) async-start(), calls=%async_computation.2 | async-start | bytes 1310720 | tf_op jit(solution)/shard_map/reduce_scatter | solution.py:346
  221.7 15.2 %collective-permute-start.14 = (bf16[1024,256]{1,0:T(8,128)(2,1)}, bf16[1024,256]{1,0:T(8,128)(2,1)}, u32[]{:S(2)}, u32[]{:S(2)}) collective-permute-start(bf16[1024,256]{1,0:T(8,128)(2,1)} %get-tuple-element.21), channel_id=1, source_target_pairs={{4,0},{0,4},{5,1},{1,5},{6,2},{2,6},{7,3},{3,7},{12,8},{8,12},{13,... | collective-permute-start | bytes 1572872 | tf_op jit(solution)/shard_map/ppermute | solution.py:34
  223.3 28.3 %collective-permute-start.16 = (bf16[1024,256]{1,0:T(8,128)(2,1)}, bf16[1024,256]{1,0:T(8,128)(2,1)}, u32[]{:S(2)}, u32[]{:S(2)}) collective-permute-start(bf16[1024,256]{1,0:T(8,128)(2,1)} %get-tuple-element.24), channel_id=1, source_target_pairs={{4,0},{0,4},{5,1},{1,5},{6,2},{2,6},{7,3},{3,7},{12,8},{8,12},{13,... | collective-permute-start | bytes 1572872 | tf_op jit(solution)/shard_map/ppermute | solution.py:34
  223.7 40.9 %collective-permute-start.18 = (bf16[1024,256]{1,0:T(8,128)(2,1)}, bf16[1024,256]{1,0:T(8,128)(2,1)}, u32[]{:S(2)}, u32[]{:S(2)}) collective-permute-start(bf16[1024,256]{1,0:T(8,128)(2,1)} %get-tuple-element.23), channel_id=1, source_target_pairs={{4,0},{0,4},{5,1},{1,5},{6,2},{2,6},{7,3},{3,7},{12,8},{8,12},{13,... | collective-permute-start | bytes 1572872 | tf_op jit(solution)/shard_map/ppermute | solution.py:34
  225.4 85.0 %collective-permute-start.20 = (bf16[1024,256]{1,0:T(8,128)(2,1)}, bf16[1024,256]{1,0:T(8,128)(2,1)S(1)}, u32[]{:S(2)}, u32[]{:S(2)}) collective-permute-start(bf16[1024,256]{1,0:T(8,128)(2,1)} %get-tuple-element.22), channel_id=1, source_target_pairs={{4,0},{0,4},{5,1},{1,5},{6,2},{2,6},{7,3},{3,7},{12,8},{8,12},{13,... | collective-permute-start | bytes 1572872 | tf_op jit(solution)/shard_map/ppermute | solution.py:34
  229.7 57.4 %collective-permute-start.5 = (bf16[1024,256]{1,0:T(8,128)(2,1)}, bf16[1024,256]{1,0:T(8,128)(2,1)}, u32[]{:S(2)}, u32[]{:S(2)}) collective-permute-start(bf16[1024,256]{1,0:T(8,128)(2,1)} %get-tuple-element.28), channel_id=1, source_target_pairs={{4,0},{0,4},{5,1},{1,5},{6,2},{2,6},{7,3},{3,7},{12,8},{8,12},{13,... | collective-permute-start | bytes 1572872 | tf_op jit(solution)/shard_map/ppermute | solution.py:34
  234.0 17.6 %copy-start.18 = (bf16[1024,256]{1,0:T(8,128)(2,1)S(1)}, bf16[1024,256]{1,0:T(8,128)(2,1)}, u32[]{:S(2)}) copy-start(bf16[1024,256]{1,0:T(8,128)(2,1)} %get-tuple-element.30) | copy-start | bytes 1572868
  236.1 53.7 %copy-start.6 = (bf16[1,1,512,4096]{3,2,1,0:T(8,128)(2,1)S(1)}, bf16[1,1,512,4096]{3,2,1,0:T(8,128)(2,1)}, u32[]{:S(2)}) copy-start(bf16[1,1,512,4096]{3,2,1,0:T(8,128)(2,1)} %param.17) | copy-start | bytes 12582916
  236.9 61.3 %collective-permute-start.7 = (bf16[1024,256]{1,0:T(8,128)(2,1)}, bf16[1024,256]{1,0:T(8,128)(2,1)S(1)}, u32[]{:S(2)}, u32[]{:S(2)}) collective-permute-start(bf16[1024,256]{1,0:T(8,128)(2,1)} %get-tuple-element.31), channel_id=1, source_target_pairs={{4,0},{0,4},{5,1},{1,5},{6,2},{2,6},{7,3},{3,7},{12,8},{8,12},{13,... | collective-permute-start | bytes 1572872 | tf_op jit(solution)/shard_map/ppermute | solution.py:34
  251.6 53.6 %collective-permute-start.9 = (bf16[1024,256]{1,0:T(8,128)(2,1)S(1)}, bf16[1024,256]{1,0:T(8,128)(2,1)S(1)}, u32[]{:S(2)}, u32[]{:S(2)}) collective-permute-start(bf16[1024,256]{1,0:T(8,128)(2,1)S(1)} %copy-done.18), channel_id=1, source_target_pairs={{4,0},{0,4},{5,1},{1,5},{6,2},{2,6},{7,3},{3,7},{12,8},{8,12},{13,... | collective-permute-start | bytes 1572872 | tf_op jit(solution)/shard_map/ppermute | solution.py:34
  266.9 43.9 %collective-permute-start.15 = (bf16[1024,256]{1,0:T(8,128)(2,1)S(1)}, bf16[1024,256]{1,0:T(8,128)(2,1)S(1)}, u32[]{:S(2)}, u32[]{:S(2)}) collective-permute-start(bf16[1024,256]{1,0:T(8,128)(2,1)S(1)} %get-tuple-element.18), channel_id=1, source_target_pairs={{3,0},{0,1},{1,2},{2,3},{7,4},{4,5},{5,6},{6,7},{11,8},{8,9},{9,10... | collective-permute-start | bytes 1572872 | tf_op jit(solution)/shard_map/ppermute | solution.py:34
  287.1 37.7 %collective-permute-start.17 = (bf16[1024,256]{1,0:T(8,128)(2,1)S(1)}, bf16[1024,256]{1,0:T(8,128)(2,1)S(1)}, u32[]{:S(2)}, u32[]{:S(2)}) collective-permute-start(bf16[1024,256]{1,0:T(8,128)(2,1)S(1)} %get-tuple-element.20), channel_id=1, source_target_pairs={{2,0},{3,1},{0,2},{1,3},{6,4},{7,5},{4,6},{5,7},{10,8},{11,9},{8,1... | collective-permute-start | bytes 1572872 | tf_op jit(solution)/shard_map/ppermute | solution.py:34
  298.2 40.8 %collective-permute-start.11 = (bf16[1024,256]{1,0:T(8,128)(2,1)S(1)}, bf16[1024,256]{1,0:T(8,128)(2,1)S(1)}, u32[]{:S(2)}, u32[]{:S(2)}) collective-permute-start(bf16[1024,256]{1,0:T(8,128)(2,1)S(1)} %copy-done.17), channel_id=1, source_target_pairs={{4,0},{0,4},{5,1},{1,5},{6,2},{2,6},{7,3},{3,7},{12,8},{8,12},{13,... | collective-permute-start | bytes 1572872 | tf_op jit(solution)/shard_map/ppermute | solution.py:34
  305.2 31.5 %collective-permute-start.19 = (bf16[1024,256]{1,0:T(8,128)(2,1)S(1)}, bf16[1024,256]{1,0:T(8,128)(2,1)S(1)}, u32[]{:S(2)}, u32[]{:S(2)}) collective-permute-start(bf16[1024,256]{1,0:T(8,128)(2,1)S(1)} %get-tuple-element.19), channel_id=1, source_target_pairs={{1,0},{2,1},{3,2},{0,3},{5,4},{6,5},{7,6},{4,7},{9,8},{10,9},{11,1... | collective-permute-start | bytes 1572872 | tf_op jit(solution)/shard_map/ppermute | solution.py:34
  310.3 14.4 %copy-start.16 = (bf16[1024,256]{1,0:T(8,128)(2,1)}, bf16[1024,256]{1,0:T(8,128)(2,1)S(1)}, u32[]{:S(2)}) copy-start(bf16[1024,256]{1,0:T(8,128)(2,1)S(1)} %collective-permute-done.20) | copy-start | bytes 1572868
  310.3 29.6 %collective-permute-start.10 = (bf16[1024,256]{1,0:T(8,128)(2,1)S(1)}, bf16[1024,256]{1,0:T(8,128)(2,1)S(1)}, u32[]{:S(2)}, u32[]{:S(2)}) collective-permute-start(bf16[1024,256]{1,0:T(8,128)(2,1)S(1)} %get-tuple-element.26), channel_id=1, source_target_pairs={{1,0},{2,1},{3,2},{0,3},{5,4},{6,5},{7,6},{4,7},{9,8},{10,9},{11,1... | collective-permute-start | bytes 1572872 | tf_op jit(solution)/shard_map/ppermute | solution.py:34
  310.8 29.1 %collective-permute-start.6 = (bf16[1024,256]{1,0:T(8,128)(2,1)S(1)}, bf16[1024,256]{1,0:T(8,128)(2,1)S(1)}, u32[]{:S(2)}, u32[]{:S(2)}) collective-permute-start(bf16[1024,256]{1,0:T(8,128)(2,1)S(1)} %get-tuple-element.25), channel_id=1, source_target_pairs={{3,0},{0,1},{1,2},{2,3},{7,4},{4,5},{5,6},{6,7},{11,8},{8,9},{9,10... | collective-permute-start | bytes 1572872 | tf_op jit(solution)/shard_map/ppermute | solution.py:34
  324.8 45.6 %collective-permute-start.8 = (bf16[1024,256]{1,0:T(8,128)(2,1)S(1)}, bf16[1024,256]{1,0:T(8,128)(2,1)S(1)}, u32[]{:S(2)}, u32[]{:S(2)}) collective-permute-start(bf16[1024,256]{1,0:T(8,128)(2,1)S(1)} %get-tuple-element.27), channel_id=1, source_target_pairs={{2,0},{3,1},{0,2},{1,3},{6,4},{7,5},{4,6},{5,7},{10,8},{11,9},{8,1... | collective-permute-start | bytes 1572872 | tf_op jit(solution)/shard_map/ppermute | solution.py:34
  (21 other events, 117.6 us)
Sparse Core Ops, SparseCore 0:
  216.7 42.1 reduce-scatter.4
  261.2 41.0 reduce-scatter.2

commit v4 on v3

--- a/solution.py
+++ b/solution.py
@@ -335,7 +335,7 @@
 
     def homed(parts, kind):
         total = parts[0].astype(f32)
-        for k in range(1, ways):
+        for k in range(1, len(parts)):
             total = total + from_ahead(parts[k].astype(kind), "mp", -k).astype(f32)
         return total
 
@@ -348,7 +348,7 @@
     def homed_scatter(parts):
         length = lax.axis_size("dp")
         dp_at = lax.axis_index("dp")
-        share = width // length
+        share = parts[0].shape[0] // length
         total = None
         for k in [*range(1, length), 0]:
             start = ((dp_at + k) % length) * share
@@ -361,13 +361,11 @@
 
     key_b = homed(gk, f32).T.astype(bf16)
     value_b = homed(gv, f32).T.astype(bf16)
-    out_grad = homed_scatter([(gate * over_rows(dy_all, a)).astype(bf16) for a in att])
-    query_grad = homed_scatter([over_rows(norm_rows, g).astype(bf16) for g in gq])
+    out_grad = scattered(homed([gate * over_rows(dy_all, a) for a in att], bf16))
+    query_grad = scattered(homed([over_rows(norm_rows, g) for g in gq], bf16))
     visual32, lat_normed, lat_rstd = norm_forward(latents.astype(f32), res_gain, res_bias)
     visual = visual32.astype(bf16)[0]
-    both = scattered(
-        over_rows(visual, jnp.concatenate([key_b, value_b], 1))
-    )
+    both = homed_scatter([over_rows(visual, jnp.concatenate([key_b, value_b], 1)).astype(bf16)])
     visual_part = (
         jnp.einsum("ni,ci->nc", key_b, w_key[0], preferred_element_type=f32)
         + jnp.einsum("ni,ci->nc", value_b, w_value[0], preferred_element_type=f32)

time: 388 us -> 381 us (0.982)
  starting transfers between devices: 54.1 us -> 18.2 us
  waiting for transfers between devices: 175 us -> 210 us
  other arithmetic: 20.8 us -> 13.3 us
  matrix products: 18.9 us -> 26 us
  local copies, waits for them, and re-layouts: 16.9 us -> 12.3 us
    ppermute x21 -> x12, starting transfers between devices: 53.9 us -> 17.9 us  [from_ahead(): return lax.ppermute(x, axis, pairs)]
    reduce_scatter x1 -> x2, waiting for transfers between devices: 0.01 us -> 31.2 us  [scattered(): lax.psum_scatter(x.astype(bf16), 'dp', scatter_dimension=0, tiled=True)]
    dot_general x5, matrix products: 13.2 us -> 20.3 us  [over_rows(): lax.dot_general(left, right, contract_rows, preferred_element_type=f32)]
    ppermute x21 -> x12, waiting for transfers between devices: 175 us -> 178 us  [from_ahead(): return lax.ppermute(x, axis, pairs)]
  transfers between devices with their start and end apart: 23 -> 15, of which waited for: 13 -> 11; matrix products, arithmetic and copies ran while one was open for 12% -> 12% of each run, Pallas kernels for 0% -> 0%
where the time goes in v4:
time: 381 us
  waiting for transfers between devices  210 us (55%)
  Pallas kernels  86.4 us (23%)
  matrix products  26 us (7%)
  starting transfers between devices  18.2 us (5%)
  between operations  14.9 us (4%)
  other arithmetic  13.3 us (3%)
  local copies, waits for them, and re-layouts  12.3 us (3%)
    ppermute x12, waiting for transfers between devices, from_ahead(): return lax.ppermute(x, axis, pairs)  178 us
    pallas_call x1, Pallas kernels, relay(): pl.pallas_call(functools.partial(relay_kernel, sections, ways), out_shape...  86.4 us
    reduce_scatter x2, waiting for transfers between devices, scattered(): lax.psum_scatter(x.astype(bf16), 'dp', scatter_dimension=0, tiled=True)  31.2 us
    dot_general x5, matrix products, over_rows(): lax.dot_general(left, right, contract_rows, preferred_element_type=f32)  20.3 us
    ppermute x12, starting transfers between devices, from_ahead(): return lax.ppermute(x, axis, pairs)  17.9 us
  transfers between devices with their start and end apart: 15, of which 11 were waited for; matrix products, arithmetic and copies ran while one was open for 12% of the time, Pallas kernels for 0%

profile of v4, /device:TPU:0, one launch (start us, length us, event | category | flops | bytes accessed | tf_op | source)
XLA Modules:
  0.0 380.6 jit_solution(3447176167777261541)
XLA Ops:
  7.3 1.1 constant_dynamic-slice_fusion.3
  8.4 3.0 collective-permute-start
  11.5 1.9 collective-permute-start.2
  13.5 1.9 collective-permute-start.4
  15.5 3.0 convert_reduce_fusion
  18.9 1.2 fusion.2
  24.3 1.3 collective-permute-done.2
  25.9 2.6 select_reduce_fusion
  28.6 2.1 fusion.10
  30.7 1.8 divide_convert_fusion.probs_ref
  36.3 34.3 %collective-permute-done.3.rest_1_ = bf16[4096,256]{1,0:T(8,128)(2,1)} collective-permute-done((bf16[4096,256]{1,0:T(8,128)(2,1)}, bf16[4096,256]{1,0:T(8,128)(2,1)}, u32[]{:S(2)}, u32[]{:S(2)}) %collective-permute-start.3) | collective-permute-done | bytes 2097184 | tf_op jit(solution)/shard_map/ppermute | solution.py:34
  70.6 44.1 %collective-permute-done.4.rest_3_ = bf16[4096,256]{1,0:T(8,128)(2,1)} collective-permute-done((bf16[4096,256]{1,0:T(8,128)(2,1)}, bf16[4096,256]{1,0:T(8,128)(2,1)}, u32[]{:S(2)}, u32[]{:S(2)}) %collective-permute-start.4) | collective-permute-done | bytes 2097184 | tf_op jit(solution)/shard_map/ppermute | solution.py:34
  114.7 86.4 %relay.1 = (bf16[512,4096]{1,0:T(8,128)(2,1)}, bf16[512,4096]{1,0:T(8,128)(2,1)}, bf16[512,512]{1,0:T(8,128)(2,1)S(1)}, f32[512,320]{1,0:T(8,128)S(1)}, f32[512,320]{1,0:T(8,128)S(1)}) custom-call(f32[1]{0:T(128)} %tanh.6.gate_ref, f32[1,4096]{1,0:T(1,128)S(1)} %copy-done.2, f32[512,1]{1,0:T(8,128)S(1)} %copy.40.mean_ref, f32[512,1]{1,0:T(8,128)S(1)} %copy.41.rstd_ref, ...), custom_call_target="tpu_custom_call" | custom-call | flops 4966055936 | bytes 25165824 | tf_op jit(solution)/shard_map/relay/pallas_call | solution.py:235
  201.1 1.7 collective-permute-start.7
  203.3 4.8 %fusion.9 = bf16[4096,256]{1,0:T(8,128)(2,1)} fusion(bf16[512,4096]{1,0:T(8,128)(2,1)} %get-tuple-element.15, f32[]{:T(128)} %bitcast.30, bf16[512,512]{0,1:T(8,128)(2,1)S(1)} %bitcast.64), kind=kOutput, calls=%fused_computation.17 | convolution fusion | flops 1075838976 | bytes 6553604 | tf_op jit(solution)/shard_map/dot_general | solution.py:343
  208.1 1.6 collective-permute-start.11
  209.7 3.5 collective-permute-done.7
  213.3 8.4 %collective-permute-done.6 = f32[256,320]{1,0:T(8,128)S(1)} collective-permute-done((f32[256,320]{1,0:T(8,128)S(1)}, f32[256,320]{1,0:T(8,128)S(1)}, u32[]{:S(2)}, u32[]{:S(2)}) %collective-permute-start.6) | collective-permute-done | bytes 327712 | tf_op jit(solution)/shard_map/ppermute | solution.py:34
  222.1 1.6 fusion.13
  223.8 38.6 %collective-permute-done.11 = bf16[4096,256]{1,0:T(8,128)(2,1)} collective-permute-done((bf16[4096,256]{1,0:T(8,128)(2,1)}, bf16[4096,256]{1,0:T(8,128)(2,1)}, u32[]{:S(2)}, u32[]{:S(2)}) %collective-permute-start.11) | collective-permute-done | bytes 2097184 | tf_op jit(solution)/shard_map/ppermute | solution.py:34
  262.3 5.6 %fusion.8 = bf16[4096,256]{1,0:T(8,128)(2,1)} fusion(bf16[512,4096]{1,0:T(8,128)(2,1)} %get-tuple-element.15, bf16[4096,256]{1,0:T(8,128)(2,1)} %collective-permute-done.11, f32[]{:T(128)} %bitcast.30, bf16[512,512]{0,1:T(8,128)(2,1)S(1)} %bitcast.65), kind=kOutput, calls=%fused_computation.16 | convolution fusion | flops 1077936128 | bytes 8650756 | tf_op jit(solution)/shard_map/dot_general | solution.py:343
  268.2 4.9 %convolution_convert_fusion = bf16[4096,256]{1,0:T(8,128)(2,1)S(1)} fusion(bf16[512,512]{1,0:T(8,128)(2,1)S(1)} %get-tuple-element.12, f32[4096]{0:T(1024)S(1)} %bitcast.88, f32[4096]{0:T(1024)S(1)} %bitcast.57, f32[512]{0:T(512)S(1)} %add_rsqrt_fusion.1, f32[512]{0:T(512)S(1)} %broadcast_multiply_fusion.1, bf16[1,1,512,4096]{3,2,1,0:T(8,128)(2,1)} %param.17), kind=kOutput, calls=%fused_computation.18 | convolution fusion | flops 1087373312 | bytes 6590464 | tf_op jit(solution)/shard_map/dot_general | solution.py:343
  273.2 2.5 collective-permute-start.5
  275.7 35.5 %collective-permute-done.5 = bf16[4096,256]{1,0:T(8,128)(2,1)S(1)} collective-permute-done((bf16[4096,256]{1,0:T(8,128)(2,1)S(1)}, bf16[4096,256]{1,0:T(8,128)(2,1)S(1)}, u32[]{:S(2)}, u32[]{:S(2)}) %collective-permute-start.5) | collective-permute-done | bytes 2097184 | tf_op jit(solution)/shard_map/ppermute | solution.py:34
  311.1 4.1 %fusion.7 = bf16[4096,256]{1,0:T(8,128)(2,1)} fusion(bf16[4096,256]{1,0:T(8,128)(2,1)S(1)} %collective-permute-done.5, bf16[512,512]{1,0:T(8,128)(2,1)S(1)} %get-tuple-element.12, f32[4096]{0:T(1024)S(1)} %bitcast.89, f32[4096]{0:T(1024)S(1)} %bitcast.58, f32[512]{0:T(512)S(1)} %add_rsqrt_fusion.1, f32[512]{0:T(512)S(1)} %broadcast_multiply_fusion.1, ...), kind=kOutput, calls=%fused_computation.15 | convolution fusion | flops 1089470464 | bytes 8687616 | tf_op jit(solution)/shard_map/dot_general | solution.py:343
  317.0 3.6 collective-permute-start.10
  321.8 2.9 collective-permute-done.10
  324.7 4.1 %collective-permute-done.8 = bf16[256,512]{1,0:T(8,128)(2,1)S(1)} collective-permute-done((bf16[256,512]{1,0:T(8,128)(2,1)S(1)}, bf16[256,512]{1,0:T(8,128)(2,1)S(1)}, u32[]{:S(2)}, u32[]{:S(2)}) %collective-permute-start.8) | collective-permute-done | bytes 262176 | tf_op jit(solution)/shard_map/ppermute | solution.py:34
  328.9 5.6 %collective-permute-done.9 = bf16[256,512]{1,0:T(8,128)(2,1)S(1)} collective-permute-done((bf16[256,512]{1,0:T(8,128)(2,1)S(1)}, bf16[256,512]{1,0:T(8,128)(2,1)S(1)}, u32[]{:S(2)}, u32[]{:S(2)}) %collective-permute-start.9) | collective-permute-done | bytes 262176 | tf_op jit(solution)/shard_map/ppermute | solution.py:34
  336.4 1.7 subtract_multiply_fusion
  338.1 31.2 %reduce-scatter.4.cloned.1.call-done = bf16[1024,256]{1,0:T(8,128)(2,1)} async-done(((bf16[4096,256]{1,0:T(8,128)(2,1)}), bf16[1024,256]{1,0:T(8,128)(2,1)}) %reduce-scatter.4.cloned.1.call-update) | async-done | bytes 524304 | tf_op jit(solution)/shard_map/reduce_scatter | solution.py:346
  369.3 4.8 %copy.47 = bf16[1,1,512,4096]{3,2,1,0:T(8,128)(2,1)} copy(bf16[1,1,512,4096]{3,2,1,0:T(8,128)(2,1)} %bitcast.60) | data formatting | bytes 8388608
  (83 shorter events, 14.4 us)
Async XLA Ops:
  7.2 214.5 %copy-start = (bf16[1,1024,256]{2,1,0:T(8,128)(2,1)S(1)}, bf16[1,1024,256]{2,1,0:T(8,128)(2,1)}, u32[]{:S(2)}) copy-start(bf16[1,1024,256]{2,1,0:T(8,128)(2,1)} %param.23) | copy-start | bytes 1572868
  7.2 328.2 %reduce-scatter.8.cloned.1.call-start = ((), (), s32[]{:S(2)}) async-start(), calls=%async_computation.5 | async-start | bytes 1474560 | tf_op jit(solution)/shard_map/reduce_scatter | solution.py:373
  8.4 17.4 %collective-permute-start = (bf16[512,256]{1,0:T(8,128)(2,1)S(1)}, bf16[512,256]{1,0:T(8,128)(2,1)S(1)}, u32[]{:S(2)}, u32[]{:S(2)}) collective-permute-start(bf16[512,256]{1,0:T(8,128)(2,1)S(1)} %get-tuple-element.22), channel_id=1, source_target_pairs={{4,0},{0,4},{5,1},{1,5},{6,2},{2,6},{7,3},{3,7},{12,8},{8,12},{13,... | collective-permute-start | bytes 786440 | tf_op jit(solution)/shard_map/ppermute | solution.py:34
  11.4 12.1 %collective-permute-start.1 = (bf16[320,256]{1,0:T(8,128)(2,1)}, bf16[320,256]{1,0:T(8,128)(2,1)S(1)}, u32[]{:S(2)}, u32[]{:S(2)}) collective-permute-start(bf16[320,256]{1,0:T(8,128)(2,1)} %bitcast.75), channel_id=1, source_target_pairs={{4,0},{0,4},{5,1},{1,5},{6,2},{2,6},{7,3},{3,7},{12,8},{8,12},{13,... | collective-permute-start | bytes 491528 | tf_op jit(solution)/shard_map/ppermute | solution.py:34
  11.5 14.1 %collective-permute-start.2 = (bf16[320,256]{1,0:T(8,128)(2,1)}, bf16[320,256]{1,0:T(8,128)(2,1)S(1)}, u32[]{:S(2)}, u32[]{:S(2)}) collective-permute-start(bf16[320,256]{1,0:T(8,128)(2,1)} %bitcast.77), channel_id=1, source_target_pairs={{4,0},{0,4},{5,1},{1,5},{6,2},{2,6},{7,3},{3,7},{12,8},{8,12},{13,... | collective-permute-start | bytes 491528 | tf_op jit(solution)/shard_map/ppermute | solution.py:34
  13.4 57.2 %collective-permute-start.3 = (bf16[4096,256]{1,0:T(8,128)(2,1)}, bf16[4096,256]{1,0:T(8,128)(2,1)}, u32[]{:S(2)}, u32[]{:S(2)}) collective-permute-start(bf16[4096,256]{1,0:T(8,128)(2,1)} %bitcast.66), channel_id=1, source_target_pairs={{4,0},{0,4},{5,1},{1,5},{6,2},{2,6},{7,3},{3,7},{12,8},{8,12},{13,... | collective-permute-start | bytes 6291464 | tf_op jit(solution)/shard_map/ppermute | solution.py:34
  13.5 101.2 %collective-permute-start.4 = (bf16[4096,256]{1,0:T(8,128)(2,1)}, bf16[4096,256]{1,0:T(8,128)(2,1)}, u32[]{:S(2)}, u32[]{:S(2)}) collective-permute-start(bf16[4096,256]{1,0:T(8,128)(2,1)} %bitcast.68), channel_id=1, source_target_pairs={{4,0},{0,4},{5,1},{1,5},{6,2},{2,6},{7,3},{3,7},{12,8},{8,12},{13,... | collective-permute-start | bytes 6291464 | tf_op jit(solution)/shard_map/ppermute | solution.py:34
  15.4 3.4 copy-start.3
  15.4 4.7 %copy-start.11 = (s32[1,1024]{1,0:T(1,128)S(1)}, s32[1,1024]{1,0:T(1,128)}, u32[]{:S(2)}) copy-start(s32[1,1024]{1,0:T(1,128)} %param.28) | copy-start | bytes 12292
  15.4 5.0 %copy-start.7 = (bf16[1,1,320,256]{3,2,1,0:T(8,128)(2,1)S(1)}, bf16[1,1,320,256]{3,2,1,0:T(8,128)(2,1)}, u32[]{:S(2)}) copy-start(bf16[1,1,320,256]{3,2,1,0:T(8,128)(2,1)} %param.26) | copy-start | bytes 491524
  15.5 5.8 %copy-start.8 = (bf16[1,1,320,256]{3,2,1,0:T(8,128)(2,1)S(1)}, bf16[1,1,320,256]{3,2,1,0:T(8,128)(2,1)}, u32[]{:S(2)}) copy-start(bf16[1,1,320,256]{3,2,1,0:T(8,128)(2,1)} %param.27) | copy-start | bytes 491524
  32.5 1.7 copy-start.5
  32.5 82.2 %copy-start.2 = (f32[1,4096]{1,0:T(1,128)S(1)}, f32[1,4096]{1,0:T(1,128)}, u32[]{:S(2)}) copy-start(f32[1,4096]{1,0:T(1,128)} %gain_ref.1) | copy-start | bytes 49156
  201.1 12.1 %collective-permute-start.7 = (f32[256,320]{1,0:T(8,128)S(1)}, f32[256,320]{1,0:T(8,128)S(1)}, u32[]{:S(2)}, u32[]{:S(2)}) collective-permute-start(f32[256,320]{1,0:T(8,128)S(1)} %split.29), channel_id=1, source_target_pairs={{4,0},{0,4},{5,1},{1,5},{6,2},{2,6},{7,3},{3,7},{12,8},{8,12},{13,... | collective-permute-start | bytes 983048 | tf_op jit(solution)/shard_map/ppermute | solution.py:34
  202.8 18.8 %collective-permute-start.6 = (f32[256,320]{1,0:T(8,128)S(1)}, f32[256,320]{1,0:T(8,128)S(1)}, u32[]{:S(2)}, u32[]{:S(2)}) collective-permute-start(f32[256,320]{1,0:T(8,128)S(1)} %split.27), channel_id=1, source_target_pairs={{4,0},{0,4},{5,1},{1,5},{6,2},{2,6},{7,3},{3,7},{12,8},{8,12},{13,... | collective-permute-start | bytes 983048 | tf_op jit(solution)/shard_map/ppermute | solution.py:34
  208.1 14.0 %copy-start.9 = (bf16[1,1024,256]{2,1,0:T(8,128)(2,1)S(1)}, bf16[1,1024,256]{2,1,0:T(8,128)(2,1)}, u32[]{:S(2)}) copy-start(bf16[1,1024,256]{2,1,0:T(8,128)(2,1)} %param.22) | copy-start | bytes 1572868
  208.1 54.2 %collective-permute-start.11 = (bf16[4096,256]{1,0:T(8,128)(2,1)}, bf16[4096,256]{1,0:T(8,128)(2,1)}, u32[]{:S(2)}, u32[]{:S(2)}) collective-permute-start(bf16[4096,256]{1,0:T(8,128)(2,1)} %fusion.9), channel_id=1, source_target_pairs={{4,0},{0,4},{5,1},{1,5},{6,2},{2,6},{7,3},{3,7},{12,8},{8,12},{13,... | collective-permute-start | bytes 6291464 | tf_op jit(solution)/shard_map/ppermute | solution.py:34
  223.7 44.5 %copy-start.12 = (f32[1,4096]{1,0:T(1,128)S(1)}, f32[1,4096]{1,0:T(1,128)}, u32[]{:S(2)}) copy-start(f32[1,4096]{1,0:T(1,128)} %param.19) | copy-start | bytes 49156
  223.7 114.4 %reduce-scatter.6.cloned.1.call-start = ((), (), s32[]{:S(2)}) async-start(), calls=%async_computation.4 | async-start | bytes 2621440 | tf_op jit(solution)/shard_map/reduce_scatter | solution.py:346
  267.9 101.4 %reduce-scatter.4.cloned.1.call-start = ((), (), s32[]{:S(2)}) async-start(), calls=%async_computation.3 | async-start | bytes 2621440 | tf_op jit(solution)/shard_map/reduce_scatter | solution.py:346
  268.2 42.9 %copy-start.4 = (bf16[1,1,512,4096]{3,2,1,0:T(8,128)(2,1)S(1)}, bf16[1,1,512,4096]{3,2,1,0:T(8,128)(2,1)}, u32[]{:S(2)}) copy-start(bf16[1,1,512,4096]{3,2,1,0:T(8,128)(2,1)} %param.17) | copy-start | bytes 12582916
  273.1 42.2 %copy-start.6 = (bf16[1,320,1024]{2,1,0:T(8,128)(2,1)S(1)}, bf16[1,320,1024]{2,1,0:T(8,128)(2,1)}, u32[]{:S(2)}) copy-start(bf16[1,320,1024]{2,1,0:T(8,128)(2,1)} %param.29) | copy-start | bytes 1966084
  273.1 42.8 %copy-start.10 = (f32[1024]{0:T(1024)S(1)}, f32[1024]{0:T(1024)}, u32[]{:S(2)}) copy-start(f32[1024]{0:T(1024)} %param.30) | copy-start | bytes 12292
  273.2 42.8 %copy-start.13 = (f32[1024]{0:T(1024)S(1)}, f32[1024]{0:T(1024)}, u32[]{:S(2)}) copy-start(f32[1024]{0:T(1024)} %param.31) | copy-start | bytes 12292
  273.2 38.0 %collective-permute-start.5 = (bf16[4096,256]{1,0:T(8,128)(2,1)S(1)}, bf16[4096,256]{1,0:T(8,128)(2,1)S(1)}, u32[]{:S(2)}, u32[]{:S(2)}) collective-permute-start(bf16[4096,256]{1,0:T(8,128)(2,1)S(1)} %convolution_convert_fusion), channel_id=1, source_target_pairs={{4,0},{0,4},{5,1},{1,5},{6,2},{2,6},{7,3},{3,7},{12,8},{8,12},{13,... | collective-permute-start | bytes 6291464 | tf_op jit(solution)/shard_map/ppermute | solution.py:34
  317.0 7.8 %collective-permute-start.10 = (bf16[256,512]{1,0:T(8,128)(2,1)S(1)}, bf16[256,512]{1,0:T(8,128)(2,1)S(1)}, u32[]{:S(2)}, u32[]{:S(2)}) collective-permute-start(bf16[256,512]{1,0:T(8,128)(2,1)S(1)} %get-tuple-element.19), channel_id=1, source_target_pairs={{1,0},{2,1},{3,2},{0,3},{5,4},{6,5},{7,6},{4,7},{9,8},{10,9},{11,1... | collective-permute-start | bytes 786440 | tf_op jit(solution)/shard_map/ppermute | solution.py:34
  320.6 8.3 %collective-permute-start.8 = (bf16[256,512]{1,0:T(8,128)(2,1)S(1)}, bf16[256,512]{1,0:T(8,128)(2,1)S(1)}, u32[]{:S(2)}, u32[]{:S(2)}) collective-permute-start(bf16[256,512]{1,0:T(8,128)(2,1)S(1)} %get-tuple-element.18), channel_id=1, source_target_pairs={{3,0},{0,1},{1,2},{2,3},{7,4},{4,5},{5,6},{6,7},{11,8},{8,9},{9,10... | collective-permute-start | bytes 786440 | tf_op jit(solution)/shard_map/ppermute | solution.py:34
  320.6 13.9 %collective-permute-start.9 = (bf16[256,512]{1,0:T(8,128)(2,1)S(1)}, bf16[256,512]{1,0:T(8,128)(2,1)S(1)}, u32[]{:S(2)}, u32[]{:S(2)}) collective-permute-start(bf16[256,512]{1,0:T(8,128)(2,1)S(1)} %get-tuple-element.20), channel_id=1, source_target_pairs={{2,0},{3,1},{0,2},{1,3},{6,4},{7,5},{4,6},{5,7},{10,8},{11,9},{8,1... | collective-permute-start | bytes 786440 | tf_op jit(solution)/shard_map/ppermute | solution.py:34
  369.3 4.8 %copy-start.1 = (bf16[1,1024,256]{2,1,0:T(8,128)(2,1)S(1)}, bf16[1,1024,256]{2,1,0:T(8,128)(2,1)}, u32[]{:S(2)}) copy-start(bf16[1,1024,256]{2,1,0:T(8,128)(2,1)} %param.23) | copy-start | bytes 1572868
Sparse Core Ops, SparseCore 0:
  223.8 40.3 reduce-scatter.7
  268.0 45.7 reduce-scatter.5
  316.8 52.4 reduce-scatter.3
